TPU v7x, 32 devices: a whole 2x2x4 slice. The times are simulated.
32 devices in a mesh: seq: 8 (over z, x), head: 4 (over y, core).
Axes of the slice: x: 2, y: 2, z: 4, core: 2. Of those that a mesh axis runs over, the one named last changes fastest.
Arguments:
- queries: bfloat16 [2048, 4096], P('seq', 'head'), may hold values from -100 to 100
- keys_values: bfloat16 [2048, 2, 512], P('seq', None, 'head'), may hold values from -4.5 to 4.5
- cache_kv: bfloat16 [2048, 2, 512], P('seq', None, 'head'), may hold values from -4 to 4
- vertical_pages: int32 [4, 4], P('head'), may hold values from 0 to 15, as said below
- slash_shift: int32 [4, 3], P('head'), may hold values from 1 to 8, as said below
- slash_live: int32 [8, 4, 3], P('seq', 'head'), may hold values 0 or 1
- out_proj: bfloat16 [4096, 2048], P('head'), may hold values from -0.09375 to 0.09375
Outputs:
- projected: bfloat16 [2048, 2048], P('seq', 'head')
Inputs may be any that keep to these rules, and one draw needn't show every extreme that they name: `vertical_pages`: each head group lists 4 distinct pages. `slash_shift`: each head group lists 3 distinct distances.
All inputs are finite; a program needn't handle non-finite values. No bound on the sum of `slash_live` on one device may be relied on, other than what follows from the above.
Results may differ from a plain program's by a relative error of at most 0.0057.
Values may be sent and summed in bfloat16 or wider, within the bound.
No kernel may reach another device: no remote copies, remote signals or barrier semaphores. Data moves between devices by JAX's collectives and lax.ppermute only.
A program may use at most 64 MiB of HBM per device.

v0:
```python
import jax
import jax.numpy as jnp
from jax import lax
from jax.sharding import PartitionSpec as P

PAGE = 128


def passed_along(value, axis, steps):
    count = lax.axis_size(axis)
    pairs = [(source, (source + steps) % count) for source in range(count)]
    return lax.ppermute(value, axis, pairs)


def rotate(stacked, amounts, shards):
    reduced = amounts % shards
    for bit_number in range(max(1, (shards - 1).bit_length())):
        moved = passed_along(stacked, "seq", 1 << bit_number)
        chosen = reduced // (1 << bit_number) % 2 == 1
        stacked = jnp.where(chosen[:, None, None, None], moved, stacked)
    return stacked


def body(queries, keys_values, cache_kv, vertical_pages, slash_shift, slash_live, out_proj):
    row_count = queries.shape[0]
    head_width = keys_values.shape[2]
    group_heads = queries.shape[1] // head_width
    shards = lax.axis_size("seq")
    own_shard = lax.axis_index("seq")
    distances = slash_shift[0]
    live_blocks = slash_live[0, 0] == 1
    page_ids = vertical_pages[0]
    slash_count = distances.shape[0]
    payload = jnp.where(
        (own_shard < shards - distances)[:, None, None, None], keys_values[None], cache_kv[None]
    )
    slash_kv = jnp.concatenate(
        [
            rotate(payload[position : position + 1], distances[position : position + 1], shards)
            for position in range(slash_count)
        ],
        0,
    )
    per_shard = row_count // PAGE
    owners = page_ids // per_shard
    whole_cache = lax.all_gather(cache_kv, "seq", axis=0, tiled=True)
    vertical = jax.vmap(
        lambda page_key: lax.dynamic_slice_in_dim(whole_cache, page_key * PAGE, PAGE, 0)
    )(page_ids)
    cached_slash = own_shard + shards - distances
    clash = (
        live_blocks[None, :]
        & (distances[None, :] > own_shard)
        & (owners[:, None] == cached_slash[None, :])
    )
    page_open = jnp.logical_not(jnp.any(clash, axis=1))
    row_ids = lax.broadcasted_iota(jnp.int32, (row_count, row_count), 0)
    col_ids = lax.broadcasted_iota(jnp.int32, (row_count, row_count), 1)
    causal = row_ids >= col_ids
    column_open = jnp.concatenate([jnp.repeat(live_blocks, row_count), jnp.repeat(page_open, PAGE)])
    visible = jnp.concatenate(
        [causal, jnp.broadcast_to(column_open[None, :], (row_count, column_open.shape[0]))], 1
    )
    all_keys = jnp.concatenate(
        [keys_values, slash_kv.reshape(-1, 2, head_width), vertical.reshape(-1, 2, head_width)], 0
    )
    query_heads = queries.reshape(row_count, group_heads, head_width)
    scores = jnp.einsum(
        "rgd,kd->grk", query_heads, all_keys[:, 0, :], preferred_element_type=jnp.float32
    )
    scores = scores * head_width ** (-0.5)
    scores = jnp.where(visible[None], scores, -jnp.inf)
    row_max = jnp.max(scores, axis=2, keepdims=True)
    weights = jnp.exp(scores - row_max)
    row_total = jnp.sum(weights, axis=2, keepdims=True)
    weights_bf = (weights / row_total).astype(jnp.bfloat16)
    attended = jnp.einsum(
        "grk,kd->rgd", weights_bf, all_keys[:, 1, :], preferred_element_type=jnp.float32
    )
    attended = attended.astype(jnp.bfloat16).reshape(row_count, group_heads * head_width)
    group_terms = jnp.dot(attended, out_proj, preferred_element_type=jnp.float32)
    return lax.psum_scatter(group_terms, "head", scatter_dimension=1, tiled=True).astype(
        jnp.bfloat16
    )


def solution(mesh):
    placed = (
        P("seq", "head"),
        P("seq", None, "head"),
        P("seq", None, "head"),
        P("head", None),
        P("head", None),
        P("seq", "head", None),
        P("head", None),
    )
    return jax.shard_map(
        body, mesh=mesh, in_specs=placed, out_specs=P("seq", "head"), check_vma=False
    )
```

profile of v0, /device:TPU:0, one launch (start us, length us, event | category | flops | bytes accessed | tf_op | source)
XLA Modules:
  0.0 124.2 jit_solution(2235613061482874402)
XLA Ops:
  6.5 0.0 copy-start
  6.5 0.0 all-gather.2.cloned.1.call-start
  6.5 0.7 all-gather.2.cloned.1.call-update
  7.3 0.0 reduce-scatter.2.cloned.1.call-start
  7.3 0.9 copy.23
  8.2 0.9 copy.25
  9.2 0.7 compare_bitcast_fusion
  9.8 0.1 broadcast_select_fusion
  10.0 3.0 %collective-permute-start = (bf16[1,256,2,128]{3,1,0,2:T(8,128)(2,1)S(1)}, bf16[1,256,2,128]{3,1,0,2:T(8,128)(2,1)S(1)}, u32[]{:S(2)}, u32[]{:S(2)}) collective-permute-start(bf16[1,256,2,128]{3,1,0,2:T(8,128)(2,1)S(1)} %get-tuple-element.8), channel_id=1, source_target_pairs={{0,4},{4,8},{8,12},{12,16},{16,20},{20,24},{24,28},{28,0},{1,5},{5... | collective-permute-start | bytes 393224 | tf_op jit(solution)/shard_map/ppermute | solution.py:12
  13.0 1.5 %collective-permute-start.6 = (bf16[1,256,2,128]{3,1,0,2:T(8,128)(2,1)S(1)}, bf16[1,256,2,128]{3,1,0,2:T(8,128)(2,1)S(1)}, u32[]{:S(2)}, u32[]{:S(2)}) collective-permute-start(bf16[1,256,2,128]{3,1,0,2:T(8,128)(2,1)S(1)} %get-tuple-element.9), channel_id=1, source_target_pairs={{0,4},{4,8},{8,12},{12,16},{16,20},{20,24},{24,28},{28,0},{1,5},{5... | collective-permute-start | bytes 393224 | tf_op jit(solution)/shard_map/ppermute | solution.py:12
  14.6 1.5 %collective-permute-start.3 = (bf16[1,256,2,128]{3,1,0,2:T(8,128)(2,1)S(1)}, bf16[1,256,2,128]{3,1,0,2:T(8,128)(2,1)S(1)}, u32[]{:S(2)}, u32[]{:S(2)}) collective-permute-start(bf16[1,256,2,128]{3,1,0,2:T(8,128)(2,1)S(1)} %get-tuple-element.10), channel_id=1, source_target_pairs={{0,4},{4,8},{8,12},{12,16},{16,20},{20,24},{24,28},{28,0},{1,5},{5... | collective-permute-start | bytes 393224 | tf_op jit(solution)/shard_map/ppermute | solution.py:12
  16.1 0.7 compare_bitcast_fusion.1
  16.7 0.7 subtract_bitcast_fusion
  17.4 0.7 and_select_fusion
  18.1 0.1 broadcast_in_dim.154
  18.2 0.2 and_reduce_fusion
  18.4 0.1 broadcast_bitcast_fusion
  18.5 0.3 pad_add_fusion
  18.7 1.4 %fusion.27 = (s32[1,1]{1,0:T(1,128)}, s32[1,1]{1,0:T(1,128)}, s32[1,1]{1,0:T(1,128)}) fusion(s32[1,3]{1,0:T(1,128)} %param.11), kind=kLoop, calls=%fused_computation.53 | loop fusion | bytes 24 | tf_op jit(solution)/shard_map/slice | solution.py:39
  25.9 0.0 collective-permute-done
  25.9 0.0 collective-permute-done.6
  25.9 0.0 collective-permute-done.3
  26.0 1.6 %collective-permute-start.1 = (bf16[1,256,2,128]{3,1,0,2:T(8,128)(2,1)S(1)}, bf16[1,256,2,128]{3,1,0,2:T(8,128)(2,1)S(1)}, u32[]{:S(2)}, u32[]{:S(2)}) collective-permute-start(bf16[1,256,2,128]{3,1,0,2:T(8,128)(2,1)S(1)} %get-tuple-element.5), channel_id=1, source_target_pairs={{0,8},{4,12},{8,16},{12,20},{16,24},{20,28},{24,0},{28,4},{1,9},{5... | collective-permute-start | bytes 393224 | tf_op jit(solution)/shard_map/ppermute | solution.py:12
  27.6 0.7 fusion.23
  28.3 1.6 %collective-permute-start.4 = (bf16[1,256,2,128]{3,1,0,2:T(8,128)(2,1)S(1)}, bf16[1,256,2,128]{3,1,0,2:T(8,128)(2,1)S(1)}, u32[]{:S(2)}, u32[]{:S(2)}) collective-permute-start(bf16[1,256,2,128]{3,1,0,2:T(8,128)(2,1)S(1)} %get-tuple-element.6), channel_id=1, source_target_pairs={{0,8},{4,12},{8,16},{12,20},{16,24},{20,28},{24,0},{28,4},{1,9},{5... | collective-permute-start | bytes 393224 | tf_op jit(solution)/shard_map/ppermute | solution.py:12
  29.9 0.3 collective-permute-start.7
  30.2 4.6 %collective-permute-done.1 = bf16[1,256,2,128]{3,1,0,2:T(8,128)(2,1)S(1)} collective-permute-done((bf16[1,256,2,128]{3,1,0,2:T(8,128)(2,1)S(1)}, bf16[1,256,2,128]{3,1,0,2:T(8,128)(2,1)S(1)}, u32[]{:S(2)}, u32[]{:S(2)}) %collective-permute-start.1) | collective-permute-done | bytes 131104 | tf_op jit(solution)/shard_map/ppermute | solution.py:12
  34.8 1.5 %collective-permute-start.2 = (bf16[1,256,2,128]{3,1,0,2:T(8,128)(2,1)S(1)}, bf16[1,256,2,128]{3,1,0,2:T(8,128)(2,1)S(1)}, u32[]{:S(2)}, u32[]{:S(2)}) collective-permute-start(bf16[1,256,2,128]{3,1,0,2:T(8,128)(2,1)S(1)} %broadcast_select_fusion.8), channel_id=1, source_target_pairs={{0,16},{4,20},{8,24},{12,28},{16,0},{20,4},{24,8},{28,12},{1,17},{... | collective-permute-start | bytes 393224 | tf_op jit(solution)/shard_map/ppermute | solution.py:12
  36.3 1.3 %collective-permute-done.4 = bf16[1,256,2,128]{3,1,0,2:T(8,128)(2,1)S(1)} collective-permute-done((bf16[1,256,2,128]{3,1,0,2:T(8,128)(2,1)S(1)}, bf16[1,256,2,128]{3,1,0,2:T(8,128)(2,1)S(1)}, u32[]{:S(2)}, u32[]{:S(2)}) %collective-permute-start.4) | collective-permute-done | bytes 131104 | tf_op jit(solution)/shard_map/ppermute | solution.py:12
  37.6 1.5 %collective-permute-start.5 = (bf16[1,256,2,128]{3,1,0,2:T(8,128)(2,1)S(1)}, bf16[1,256,2,128]{3,1,0,2:T(8,128)(2,1)S(1)}, u32[]{:S(2)}, u32[]{:S(2)}) collective-permute-start(bf16[1,256,2,128]{3,1,0,2:T(8,128)(2,1)S(1)} %broadcast_select_fusion.5), channel_id=1, source_target_pairs={{0,16},{4,20},{8,24},{12,28},{16,0},{20,4},{24,8},{28,12},{1,17},{... | collective-permute-start | bytes 393224 | tf_op jit(solution)/shard_map/ppermute | solution.py:12
  39.1 1.3 %collective-permute-done.7 = bf16[1,256,2,128]{3,1,0,2:T(8,128)(2,1)S(1)} collective-permute-done((bf16[1,256,2,128]{3,1,0,2:T(8,128)(2,1)S(1)}, bf16[1,256,2,128]{3,1,0,2:T(8,128)(2,1)S(1)}, u32[]{:S(2)}, u32[]{:S(2)}) %collective-permute-start.7) | collective-permute-done | bytes 131104 | tf_op jit(solution)/shard_map/ppermute | solution.py:12
  40.4 8.5 %collective-permute-start.8 = (bf16[1,256,2,128]{3,1,0,2:T(8,128)(2,1)S(1)}, bf16[1,256,2,128]{3,1,0,2:T(8,128)(2,1)S(1)}, u32[]{:S(2)}, u32[]{:S(2)}) collective-permute-start(bf16[1,256,2,128]{3,1,0,2:T(8,128)(2,1)S(1)} %broadcast_select_fusion.2), channel_id=1, source_target_pairs={{0,16},{4,20},{8,24},{12,28},{16,0},{20,4},{24,8},{28,12},{1,17},{... | collective-permute-start | bytes 393224 | tf_op jit(solution)/shard_map/ppermute | solution.py:12
  49.0 0.7 collective-permute-done.2
  49.7 4.2 %collective-permute-done.5 = bf16[1,256,2,128]{3,1,0,2:T(8,128)(2,1)S(1)} collective-permute-done((bf16[1,256,2,128]{3,1,0,2:T(8,128)(2,1)S(1)}, bf16[1,256,2,128]{3,1,0,2:T(8,128)(2,1)S(1)}, u32[]{:S(2)}, u32[]{:S(2)}) %collective-permute-start.5) | collective-permute-done | bytes 131104 | tf_op jit(solution)/shard_map/ppermute | solution.py:12
  53.9 6.4 %collective-permute-done.8 = bf16[1,256,2,128]{3,1,0,2:T(8,128)(2,1)S(1)} collective-permute-done((bf16[1,256,2,128]{3,1,0,2:T(8,128)(2,1)S(1)}, bf16[1,256,2,128]{3,1,0,2:T(8,128)(2,1)S(1)}, u32[]{:S(2)}, u32[]{:S(2)}) %collective-permute-start.8) | collective-permute-done | bytes 131104 | tf_op jit(solution)/shard_map/ppermute | solution.py:12
  60.4 7.5 %all-gather.2.cloned.1.call-done = bf16[2048,2,128]{2,1,0:T(2,128)(2,1)} async-done(((bf16[256,2,128]{2,1,0:T(2,128)(2,1)}), bf16[2048,2,128]{2,1,0:T(2,128)(2,1)}) %all-gather.2.cloned.1.call-update) | async-done | bytes 1048592 | tf_op jit(solution)/shard_map/all_gather | solution.py:46
  67.8 2.3 %gather_fusion = bf16[4,128,2,128]{3,2,1,0:T(2,128)(2,1)S(1)} fusion(bf16[2048,2,128]{2,1,0:T(2,128)(2,1)} %all-gather.2.cloned.1.call-done, s32[4]{0:T(128)S(1)} %fusion.23), kind=kCustom, calls=%fused_computation | custom fusion | bytes 524336 | tf_op jit(solution)/shard_map/vmap()/gather | solution.py:48
  70.2 0.1 pad_maximum_fusion
  70.2 0.0 copy-done
  70.3 6.9 %fusion.28 = (f32[8,256]{1,0:T(8,128)S(1)}, f32[8,256,1536]{1,2,0:T(8,128)}) fusion(pred[256,1536]{0,1:T(8,128)(4,1)S(1)} %pad_add_fusion, bf16[1536,2,128]{2,0,1:T(8,128)(2,1)S(1)} %pad_maximum_fusion, bf16[256,1024]{1,0:T(8,128)(2,1)S(1)} %copy-done), kind=kOutput, calls=%fused_computation.54 | convolution fusion | flops 817890816 | bytes 13901824 | tf_op jit(solution)/shard_map/sub | solution.py:74
  77.2 0.0 copy-start.1
  77.2 5.7 %fusion.8 = bf16[128,8,256]{2,0,1:T(8,128)(2,1)S(1)} fusion(f32[8,256,1536]{1,2,0:T(8,128)} %get-tuple-element.17, f32[8,256]{1,0:T(8,128)S(1)} %get-tuple-element.16, bf16[1536,2,128]{2,0,1:T(8,128)(2,1)S(1)} %pad_maximum_fusion), kind=kOutput, calls=%fused_computation.12 | convolution fusion | flops 811859968 | bytes 13508608 | tf_op jit(solution)/shard_map/grk,kd->rgd/dot_general | solution.py:77
  82.9 0.0 copy-done.1
  83.0 2.6 %fusion.33 = f32[256,2048]{1,0:T(8,128)} fusion(bf16[256,1024]{0,1:T(8,128)(2,1)S(1)} %bitcast.95, bf16[1024,2048]{1,0:T(8,128)(2,1)S(1)} %copy-done.1), kind=kOutput, calls=%fused_computation.55 | convolution fusion | flops 1073741824 | bytes 6815744 | tf_op jit(solution)/shard_map/dot_general | solution.py:81
  85.6 0.0 reduce-scatter.2.cloned.1.call-update
  85.6 30.0 %reduce-scatter.2.cloned.1.call-done = f32[256,512]{1,0:T(8,128)} async-done(((f32[256,2048]{1,0:T(8,128)}), f32[256,512]{1,0:T(8,128)}) %reduce-scatter.2.cloned.1.call-update) | async-done | bytes 524304 | tf_op jit(solution)/shard_map/reduce_scatter | solution.py:82
  115.6 1.8 %convert_element_type.15 = bf16[256,512]{1,0:T(8,128)(2,1)} convert(f32[256,512]{1,0:T(8,128)} %reduce-scatter.2.cloned.1.call-done) | non-fusion elementwise | flops 131072 | bytes 786432 | tf_op jit(solution)/shard_map/convert_element_type | solution.py:82
  (15 shorter events, 0.3 us)
Async XLA Ops:
  6.5 63.7 %copy-start = (bf16[256,1024]{1,0:T(8,128)(2,1)S(1)}, bf16[256,1024]{1,0:T(8,128)(2,1)}, u32[]{:S(2)}) copy-start(bf16[256,1024]{1,0:T(8,128)(2,1)} %param.7) | copy-start | bytes 1572868
  6.5 61.3 %all-gather.2.cloned.1.call-start = ((), (), s32[]{:S(2)}) async-start(), calls=%async_computation.1 | async-start | bytes 1179648 | tf_op jit(solution)/shard_map/all_gather | solution.py:46
  7.3 108.3 %reduce-scatter.2.cloned.1.call-start = ((), (), s32[]{:S(2)}) async-start(), calls=%async_computation.2 | async-start | bytes 2621440 | tf_op jit(solution)/shard_map/reduce_scatter | solution.py:82
  10.0 15.9 %collective-permute-start = (bf16[1,256,2,128]{3,1,0,2:T(8,128)(2,1)S(1)}, bf16[1,256,2,128]{3,1,0,2:T(8,128)(2,1)S(1)}, u32[]{:S(2)}, u32[]{:S(2)}) collective-permute-start(bf16[1,256,2,128]{3,1,0,2:T(8,128)(2,1)S(1)} %get-tuple-element.8), channel_id=1, source_target_pairs={{0,4},{4,8},{8,12},{12,16},{16,20},{20,24},{24,28},{28,0},{1,5},{5... | collective-permute-start | bytes 393224 | tf_op jit(solution)/shard_map/ppermute | solution.py:12
  13.0 12.9 %collective-permute-start.6 = (bf16[1,256,2,128]{3,1,0,2:T(8,128)(2,1)S(1)}, bf16[1,256,2,128]{3,1,0,2:T(8,128)(2,1)S(1)}, u32[]{:S(2)}, u32[]{:S(2)}) collective-permute-start(bf16[1,256,2,128]{3,1,0,2:T(8,128)(2,1)S(1)} %get-tuple-element.9), channel_id=1, source_target_pairs={{0,4},{4,8},{8,12},{12,16},{16,20},{20,24},{24,28},{28,0},{1,5},{5... | collective-permute-start | bytes 393224 | tf_op jit(solution)/shard_map/ppermute | solution.py:12
  14.6 11.4 %collective-permute-start.3 = (bf16[1,256,2,128]{3,1,0,2:T(8,128)(2,1)S(1)}, bf16[1,256,2,128]{3,1,0,2:T(8,128)(2,1)S(1)}, u32[]{:S(2)}, u32[]{:S(2)}) collective-permute-start(bf16[1,256,2,128]{3,1,0,2:T(8,128)(2,1)S(1)} %get-tuple-element.10), channel_id=1, source_target_pairs={{0,4},{4,8},{8,12},{12,16},{16,20},{20,24},{24,28},{28,0},{1,5},{5... | collective-permute-start | bytes 393224 | tf_op jit(solution)/shard_map/ppermute | solution.py:12
  26.0 8.8 %collective-permute-start.1 = (bf16[1,256,2,128]{3,1,0,2:T(8,128)(2,1)S(1)}, bf16[1,256,2,128]{3,1,0,2:T(8,128)(2,1)S(1)}, u32[]{:S(2)}, u32[]{:S(2)}) collective-permute-start(bf16[1,256,2,128]{3,1,0,2:T(8,128)(2,1)S(1)} %get-tuple-element.5), channel_id=1, source_target_pairs={{0,8},{4,12},{8,16},{12,20},{16,24},{20,28},{24,0},{28,4},{1,9},{5... | collective-permute-start | bytes 393224 | tf_op jit(solution)/shard_map/ppermute | solution.py:12
  28.3 9.3 %collective-permute-start.4 = (bf16[1,256,2,128]{3,1,0,2:T(8,128)(2,1)S(1)}, bf16[1,256,2,128]{3,1,0,2:T(8,128)(2,1)S(1)}, u32[]{:S(2)}, u32[]{:S(2)}) collective-permute-start(bf16[1,256,2,128]{3,1,0,2:T(8,128)(2,1)S(1)} %get-tuple-element.6), channel_id=1, source_target_pairs={{0,8},{4,12},{8,16},{12,20},{16,24},{20,28},{24,0},{28,4},{1,9},{5... | collective-permute-start | bytes 393224 | tf_op jit(solution)/shard_map/ppermute | solution.py:12
  29.9 10.5 %collective-permute-start.7 = (bf16[1,256,2,128]{3,1,0,2:T(8,128)(2,1)S(1)}, bf16[1,256,2,128]{3,1,0,2:T(8,128)(2,1)S(1)}, u32[]{:S(2)}, u32[]{:S(2)}) collective-permute-start(bf16[1,256,2,128]{3,1,0,2:T(8,128)(2,1)S(1)} %get-tuple-element.7), channel_id=1, source_target_pairs={{0,8},{4,12},{8,16},{12,20},{16,24},{20,28},{24,0},{28,4},{1,9},{5... | collective-permute-start | bytes 393224 | tf_op jit(solution)/shard_map/ppermute | solution.py:12
  34.8 14.8 %collective-permute-start.2 = (bf16[1,256,2,128]{3,1,0,2:T(8,128)(2,1)S(1)}, bf16[1,256,2,128]{3,1,0,2:T(8,128)(2,1)S(1)}, u32[]{:S(2)}, u32[]{:S(2)}) collective-permute-start(bf16[1,256,2,128]{3,1,0,2:T(8,128)(2,1)S(1)} %broadcast_select_fusion.8), channel_id=1, source_target_pairs={{0,16},{4,20},{8,24},{12,28},{16,0},{20,4},{24,8},{28,12},{1,17},{... | collective-permute-start | bytes 393224 | tf_op jit(solution)/shard_map/ppermute | solution.py:12
  37.6 16.2 %collective-permute-start.5 = (bf16[1,256,2,128]{3,1,0,2:T(8,128)(2,1)S(1)}, bf16[1,256,2,128]{3,1,0,2:T(8,128)(2,1)S(1)}, u32[]{:S(2)}, u32[]{:S(2)}) collective-permute-start(bf16[1,256,2,128]{3,1,0,2:T(8,128)(2,1)S(1)} %broadcast_select_fusion.5), channel_id=1, source_target_pairs={{0,16},{4,20},{8,24},{12,28},{16,0},{20,4},{24,8},{28,12},{1,17},{... | collective-permute-start | bytes 393224 | tf_op jit(solution)/shard_map/ppermute | solution.py:12
  40.4 19.8 %collective-permute-start.8 = (bf16[1,256,2,128]{3,1,0,2:T(8,128)(2,1)S(1)}, bf16[1,256,2,128]{3,1,0,2:T(8,128)(2,1)S(1)}, u32[]{:S(2)}, u32[]{:S(2)}) collective-permute-start(bf16[1,256,2,128]{3,1,0,2:T(8,128)(2,1)S(1)} %broadcast_select_fusion.2), channel_id=1, source_target_pairs={{0,16},{4,20},{8,24},{12,28},{16,0},{20,4},{24,8},{28,12},{1,17},{... | collective-permute-start | bytes 393224 | tf_op jit(solution)/shard_map/ppermute | solution.py:12
  77.2 5.8 %copy-start.1 = (bf16[1024,2048]{1,0:T(8,128)(2,1)S(1)}, bf16[1024,2048]{1,0:T(8,128)(2,1)}, u32[]{:S(2)}) copy-start(bf16[1024,2048]{1,0:T(8,128)(2,1)} %param.13) | copy-start | bytes 12582916
Sparse Core Ops, SparseCore 0:
  9.5 58.3 all-gather.1
  85.7 29.8 reduce-scatter.1
where the time goes:
time: 125 us; the launch traced here: 124 us
  waiting for transfers between devices  56.7 us (45%)
  starting transfers between devices  21.1 us (17%)
  between operations  19.4 us (16%)
  matrix products  15.3 us (12%)
  other arithmetic  5.95 us (5%)
  local copies, waits for them, and re-layouts  5.8 us (5%)
    reduce_scatter x1, waiting for transfers between devices, body(): lax.psum_scatter(group_terms, 'head', scatter_dimension=1, tiled=True)  30 us
    ppermute x9, starting transfers between devices, passed_along(): return lax.ppermute(value, axis, pairs)  21.1 us
    ppermute x9, waiting for transfers between devices, passed_along(): return lax.ppermute(value, axis, pairs)  18.5 us
    all_gather x1, waiting for transfers between devices, body(): whole_cache = lax.all_gather(cache_kv, 'seq', axis=0, tiled=True)  7.47 us
    sub x1, matrix products, body(): weights = jnp.exp(scores - row_max)  6.94 us
    dot_general x1, matrix products, body(): jnp.einsum('grk,kd->rgd', weights_bf, all_keys[:, 1, :], preferred_elemen...  5.73 us
    dot_general x1, matrix products, body(): jnp.dot(attended, out_proj, preferred_element_type=jnp.float32)  2.61 us
  transfers between devices with their start and end apart: 11, of which 8 were waited for; matrix products, arithmetic and copies ran while one was open for 6% of the time, Pallas kernels for 0%

commit v1 on v0

v1 whole, which is shorter than its diff:
```python
import functools
import math

import jax
import jax.numpy as jnp
from jax import lax
from jax.experimental import pallas as pl
from jax.experimental.pallas import tpu as pltpu
from jax.sharding import PartitionSpec as P

PAGE = 128
LANES = 128
FAR = 1e30
TREE_MAX = 16


def swapped(value, axis, mask):
    count = lax.axis_size(axis)
    return lax.ppermute(value, axis, [(source, source ^ mask) for source in range(count)])


def passed_along(value, axis, steps):
    count = lax.axis_size(axis)
    return lax.ppermute(value, axis, [(source, (source + steps) % count) for source in range(count)])


def gathered(own, axis):
    blocks = {0: own}
    for mask in range(1, lax.axis_size(axis)):
        low = mask & -mask
        blocks[mask] = swapped(blocks[mask - low], axis, low)
    return [blocks[mask] for mask in range(len(blocks))]


def rotate(value, amount, shards):
    reduced = amount % shards
    for bit_number in range(max(1, (shards - 1).bit_length())):
        moved = passed_along(value, "seq", 1 << bit_number)
        value = jnp.where(reduced // (1 << bit_number) % 2 == 1, moved, value)
    return value


def attention_kernel(sizes, page_ref, shift_ref, live_ref, query_ref, own_ref, proj_ref, *rest):
    (shards, heads, head_width, slash_count, page_count, page_rows, per_shard, members, tree) = sizes
    store_count = (2 * shards - 1) if tree else (slash_count + page_count)
    stores = rest[:store_count]
    send_ref, keep_ref = rest[store_count : store_count + 2]
    raw, wide, keys, values, scores, weights, attended, proj, sems, proj_sem = rest[store_count + 2 :]
    me = lax.axis_index("seq")
    rows = query_ref.shape[0]
    proj_copy = pltpu.make_async_copy(proj_ref, proj, proj_sem)
    proj_copy.start()

    def slot(number):
        if number < slash_count:
            return raw.at[pl.ds(number * 2 * rows, 2 * rows)]
        first = slash_count * 2 * rows + (number - slash_count) * 2 * page_rows
        return raw.at[pl.ds(first, 2 * page_rows)]

    live = []
    for k in range(slash_count):
        distance = shift_ref[0, k]
        live.append((live_ref[0, k] == 1, distance > me, shards + me - distance))
        if not tree:
            pltpu.make_async_copy(stores[k], slot(k), sems.at[k]).start()
            continue
        differs = jnp.where(distance > me, shards + me - distance, me - distance) ^ me
        for mask in range(shards):
            for newer in (False, True):
                if newer and mask == 0:
                    continue
                source = stores[shards + mask - 1] if newer else stores[mask]

                @pl.when((differs == mask) & ((distance <= me) == newer))
                def _(source=source):
                    pltpu.make_async_copy(source, slot(k), sems.at[k]).start()

    opened = []
    for i in range(page_count):
        page = page_ref[0, i]
        owner = page // per_shard
        clash = functools.reduce(
            jnp.logical_or, [is_live & older & (source == owner) for is_live, older, source in live]
        )
        opened.append(jnp.logical_not(clash))
        number = slash_count + i
        if not tree:
            pltpu.make_async_copy(stores[number], slot(number), sems.at[number]).start()
            continue
        first = pl.multiple_of((page - owner * per_shard) * 2 * page_rows, 2 * page_rows)
        for mask in range(shards):

            @pl.when((owner ^ me) == mask)
            def _(mask=mask):
                pltpu.make_async_copy(
                    stores[mask].at[pl.ds(first, 2 * page_rows)], slot(number), sems.at[number]
                ).start()

    def split(source, first, count):
        wide[pl.ds(2 * first, 2 * count), :] = source[...].astype(jnp.float32)
        keys[pl.ds(first, count), :] = wide[pl.ds(2 * first, count, stride=2), :].astype(jnp.bfloat16)
        values[pl.ds(first, count), pl.ds(0, head_width)] = wide[
            pl.ds(2 * first + 1, count, stride=2), :
        ].astype(jnp.bfloat16)

    values[:, pl.ds(head_width, LANES)] = jnp.ones((values.shape[0], LANES), jnp.bfloat16)
    split(own_ref, 0, rows)
    chunks = [(0, rows, None)]
    first = rows
    for number in range(slash_count + page_count):
        count = rows if number < slash_count else page_rows
        place = slot(number)
        pltpu.make_async_copy(place, place, sems.at[number]).wait()
        split(place, first, count)
        flag = live[number][0] if number < slash_count else opened[number - slash_count]
        chunks.append((first, count, flag))
        first += count
    scale = head_width**-0.5 * math.log2(math.e)
    causal = lax.broadcasted_iota(jnp.int32, (rows, rows), 0) >= lax.broadcasted_iota(
        jnp.int32, (rows, rows), 1
    )

    def one_head(head, carry):
        column = pl.multiple_of(head * head_width, head_width)
        query = query_ref[:, pl.ds(column, head_width)]
        highest = None
        for start, count, flag in chunks:
            part = lax.dot_general(
                query,
                keys[pl.ds(start, count), :],
                (((1,), (1,)), ((), ())),
                preferred_element_type=jnp.float32,
            )
            if flag is None:
                part = jnp.where(causal, part, -FAR)
            scores[:, pl.ds(start, count)] = part
            top = functools.reduce(
                jnp.maximum, [part[:, at : at + LANES] for at in range(0, count, LANES)]
            )
            if flag is not None:
                top = jnp.where(flag, top, -FAR)
            highest = top if highest is None else jnp.maximum(highest, top)
        highest = jnp.max(highest, axis=1, keepdims=True)
        for start, count, flag in chunks:
            level = highest if flag is None else jnp.where(flag, highest, FAR)
            part = jnp.exp2((scores[:, pl.ds(start, count)] - level) * scale)
            weights[:, pl.ds(start, count)] = part.astype(jnp.bfloat16)
        total = jnp.dot(weights[...], values[...], preferred_element_type=jnp.float32)
        attended[:, pl.ds(column, head_width)] = (
            total[:, :head_width] / total[:, head_width:]
        ).astype(jnp.bfloat16)
        return carry

    lax.fori_loop(0, heads, one_head, 0)
    proj_copy.wait()
    mine = lax.axis_index("head")
    block = proj_ref.shape[1] // members
    for mask in range(members):
        column = pl.multiple_of((mine ^ mask) * block, block)
        term = jnp.dot(attended[...], proj[:, pl.ds(column, block)], preferred_element_type=jnp.float32)
        if mask % 2:
            send_ref[mask // 2] = term.astype(send_ref.dtype)
        else:
            keep_ref[mask // 2] = term


def body(queries, keys_values, cache_kv, vertical_pages, slash_shift, slash_live, out_proj):
    row_count = queries.shape[0]
    head_width = keys_values.shape[2]
    heads = queries.shape[1] // head_width
    shards = lax.axis_size("seq")
    members = lax.axis_size("head")
    slash_count = slash_shift.shape[1]
    page_count = vertical_pages.shape[1]
    per_shard = row_count // PAGE
    out_width = out_proj.shape[1]
    own = keys_values.reshape(2 * row_count, head_width)
    tree = shards <= TREE_MAX and shards & (shards - 1) == 0
    if tree:
        cache = cache_kv.reshape(2 * row_count, head_width)
        stores = gathered(cache, "seq") + gathered(own, "seq")[1:]
    else:
        own_shard = lax.axis_index("seq")
        stores = []
        for k in range(slash_count):
            distance = slash_shift[0, k]
            payload = jnp.where(own_shard < shards - distance, keys_values, cache_kv)
            stores.append(rotate(payload, distance, shards).reshape(2 * row_count, head_width))
        whole = lax.all_gather(cache_kv, "seq", axis=0, tiled=True)
        for i in range(page_count):
            page = lax.dynamic_slice_in_dim(whole, vertical_pages[0, i] * PAGE, PAGE, 0)
            stores.append(page.reshape(2 * PAGE, head_width))
    key_count = (1 + slash_count) * row_count + page_count * PAGE
    slots = slash_count + page_count
    sizes = (
        shards, heads, head_width, slash_count, page_count, PAGE, per_shard, members, tree,
    )
    anywhere = pl.BlockSpec(memory_space=pl.ANY)
    scalars = pl.BlockSpec(memory_space=pltpu.SMEM)
    vector = pl.BlockSpec(memory_space=pltpu.VMEM)
    block = out_width // members
    send, keep = pl.pallas_call(
        functools.partial(attention_kernel, sizes),
        out_shape=[
            jax.ShapeDtypeStruct((members // 2, row_count, block), jnp.bfloat16),
            jax.ShapeDtypeStruct((members // 2, row_count, block), jnp.float32),
        ],
        in_specs=[scalars] * 3 + [vector, vector, anywhere] + [anywhere] * len(stores),
        out_specs=[vector, vector],
        scratch_shapes=[
            pltpu.VMEM((2 * (key_count - row_count), head_width), jnp.bfloat16),
            pltpu.VMEM((2 * key_count, head_width), jnp.float32),
            pltpu.VMEM((key_count, head_width), jnp.bfloat16),
            pltpu.VMEM((key_count, head_width + LANES), jnp.bfloat16),
            pltpu.VMEM((row_count, key_count), jnp.float32),
            pltpu.VMEM((row_count, key_count), jnp.bfloat16),
            pltpu.VMEM((row_count, heads * head_width), jnp.bfloat16),
            pltpu.VMEM(out_proj.shape, jnp.bfloat16),
            pltpu.SemaphoreType.DMA((slots,)),
            pltpu.SemaphoreType.DMA,
        ],
        compiler_params=pltpu.CompilerParams(vmem_limit_bytes=24 << 20),
        cost_estimate=pl.CostEstimate(
            flops=4 * heads * row_count * key_count * head_width
            + 2 * row_count * heads * head_width * out_width,
            bytes_accessed=8 << 20,
            transcendentals=heads * row_count * key_count,
        ),
        name="attend",
    )(
        vertical_pages,
        slash_shift,
        slash_live.reshape(1, slash_count),
        queries,
        own,
        out_proj,
        *stores,
    )
    step = 1
    while step < members:
        keep = keep + swapped(send, "head", step).astype(jnp.float32)
        step *= 2
        if step < members:
            send = keep[1::2].astype(jnp.bfloat16)
            keep = keep[0::2]
    return keep[0].astype(jnp.bfloat16)


def solution(mesh):
    placed = (
        P("seq", "head"),
        P("seq", None, "head"),
        P("seq", None, "head"),
        P("head", None),
        P("head", None),
        P("seq", "head", None),
        P("head", None),
    )
    return jax.shard_map(
        body, mesh=mesh, in_specs=placed, out_specs=P("seq", "head"), check_vma=False
    )
```

time: 125 us -> 65.9 us (0.53)
  waiting for transfers between devices: 56.7 us -> 24.8 us
  between operations: 19.4 us -> 0.06 us
  matrix products: 15.3 us -> 0 us
  Pallas kernels: 0 us -> 13.5 us
  other arithmetic: 5.95 us -> 0.95 us
  starting transfers between devices: 21.1 us -> 19.3 us
    reduce_scatter x1 -> x0, waiting for transfers between devices: 30 us -> none  [body(): lax.psum_scatter(group_terms, 'head', scatter_dimension=1, tiled=True)]
    pallas_call x0 -> x1, Pallas kernels: none -> 13.5 us  [body(): pl.pallas_call(functools.partial(attention_kernel, sizes), out_shape=[jax...]
    dot_general x2 -> x0, matrix products: 8.35 us -> none  [the longest x1 5.73 us: body(): jnp.einsum('grk,kd->rgd', weights_bf, all_keys[:, 1, :], preferred_elemen...]
    all_gather x1 -> x0, waiting for transfers between devices: 7.47 us -> none  [body(): whole_cache = lax.all_gather(cache_kv, 'seq', axis=0, tiled=True)]
    sub x1 -> x0, matrix products: 6.94 us -> none  [body(): weights = jnp.exp(scores - row_max)]
    ppermute x9 -> x16, waiting for transfers between devices: 18.5 us -> 24.8 us  [swapped(): lax.ppermute(value, axis, [(source, source ^ mask) for source in range(co...]
    unnamed x6 -> x14, local copies, waits for them, and re-layouts: 1.88 us -> 7 us
    gather x2 -> x0, local copies, waits for them, and re-layouts: 2.33 us -> none  [body(): lax.dynamic_slice_in_dim(whole_cache, page_key * PAGE, PAGE, 0)]
  transfers between devices with their start and end apart: 11 -> 16, of which waited for: 8 -> 10; matrix products, arithmetic and copies ran while one was open for 6% -> 0% of each run, Pallas kernels for 0% -> 0%
where the time goes in v1:
time: 65.9 us; the launch traced here: 65.6 us
  waiting for transfers between devices  24.8 us (38%)
  starting transfers between devices  19.3 us (29%)
  Pallas kernels  13.5 us (20%)
  local copies, waits for them, and re-layouts  7.03 us (11%)
  other arithmetic  0.95 us (1%)
    ppermute x16, waiting for transfers between devices, swapped(): lax.ppermute(value, axis, [(source, source ^ mask) for source in range(co...  24.8 us
    ppermute x16, starting transfers between devices, swapped(): lax.ppermute(value, axis, [(source, source ^ mask) for source in range(co...  19.3 us
    pallas_call x1, Pallas kernels, body(): pl.pallas_call(functools.partial(attention_kernel, sizes), out_shape=[jax...  13.5 us
    unnamed x14, local copies, waits for them, and re-layouts  7 us
  transfers between devices with their start and end apart: 16, of which 10 were waited for; matrix products, arithmetic and copies ran while one was open for 0% of the time, Pallas kernels for 0%

profile of v1, /device:TPU:0, one launch (start us, length us, event | category | flops | bytes accessed | tf_op | source)
XLA Modules:
  0.0 65.6 jit_solution(12854312999020276926)
XLA Ops:
  0.0 4.1 %collective-permute-start.10 = (bf16[512,128]{1,0:T(8,128)(2,1)}, bf16[512,128]{1,0:T(8,128)(2,1)S(1)}, u32[]{:S(2)}, u32[]{:S(2)}) collective-permute-start(bf16[512,128]{1,0:T(8,128)(2,1)} %bitcast.5), channel_id=1, source_target_pairs={{0,16},{4,20},{8,24},{12,28},{16,0},{20,4},{24,8},{28,12},{1,17},{... | collective-permute-start | bytes 393224 | tf_op jit(solution)/shard_map/ppermute | solution.py:19
  4.1 1.6 %collective-permute-start.8 = (bf16[512,128]{1,0:T(8,128)(2,1)}, bf16[512,128]{1,0:T(8,128)(2,1)S(1)}, u32[]{:S(2)}, u32[]{:S(2)}) collective-permute-start(bf16[512,128]{1,0:T(8,128)(2,1)} %bitcast.6), channel_id=1, source_target_pairs={{0,8},{4,12},{8,0},{12,4},{16,24},{20,28},{24,16},{28,20},{1,9},{5... | collective-permute-start | bytes 393224 | tf_op jit(solution)/shard_map/ppermute | solution.py:19
  5.6 1.5 %collective-permute-start.7 = (bf16[512,128]{1,0:T(8,128)(2,1)}, bf16[512,128]{1,0:T(8,128)(2,1)S(1)}, u32[]{:S(2)}, u32[]{:S(2)}) collective-permute-start(bf16[512,128]{1,0:T(8,128)(2,1)} %bitcast.7), channel_id=1, source_target_pairs={{0,4},{4,0},{8,12},{12,8},{16,20},{20,16},{24,28},{28,24},{1,5},{5... | collective-permute-start | bytes 393224 | tf_op jit(solution)/shard_map/ppermute | solution.py:19
  7.1 0.3 collective-permute-start.3
  7.5 0.4 collective-permute-start.1
  7.9 4.0 %collective-permute-done.10.rest_11_ = bf16[512,128]{1,0:T(8,128)(2,1)S(1)} collective-permute-done((bf16[512,128]{1,0:T(8,128)(2,1)}, bf16[512,128]{1,0:T(8,128)(2,1)S(1)}, u32[]{:S(2)}, u32[]{:S(2)}) %collective-permute-start.10) | collective-permute-done | bytes 131104 | tf_op jit(solution)/shard_map/ppermute | solution.py:19
  11.9 2.4 %collective-permute-start = (bf16[512,128]{1,0:T(8,128)(2,1)}, bf16[512,128]{1,0:T(8,128)(2,1)S(1)}, u32[]{:S(2)}, u32[]{:S(2)}) collective-permute-start(bf16[512,128]{1,0:T(8,128)(2,1)} %bitcast.11), channel_id=1, source_target_pairs={{0,4},{4,0},{8,12},{12,8},{16,20},{20,16},{24,28},{28,24},{1,5},{5... | collective-permute-start | bytes 393224 | tf_op jit(solution)/shard_map/ppermute | solution.py:19
  14.3 0.0 collective-permute-done.8.rest_9_
  14.3 0.0 collective-permute-start.12
  14.3 0.0 collective-permute-done.7.rest_8_
  14.3 0.6 collective-permute-start.11
  15.0 1.3 %collective-permute-done.3.rest_4_ = bf16[512,128]{1,0:T(8,128)(2,1)S(1)} collective-permute-done((bf16[512,128]{1,0:T(8,128)(2,1)}, bf16[512,128]{1,0:T(8,128)(2,1)S(1)}, u32[]{:S(2)}, u32[]{:S(2)}) %collective-permute-start.3) | collective-permute-done | bytes 131104 | tf_op jit(solution)/shard_map/ppermute | solution.py:19
  16.3 0.7 %collective-permute-start.5 = (bf16[512,128]{1,0:T(8,128)(2,1)S(1)}, bf16[512,128]{1,0:T(8,128)(2,1)S(1)}, u32[]{:S(2)}, u32[]{:S(2)}) collective-permute-start(bf16[512,128]{1,0:T(8,128)(2,1)S(1)} %collective-permute-done.3.rest_4_), channel_id=1, source_target_pairs={{0,8},{4,12},{8,0},{12,4},{16,24},{20,28},{24,16},{28,20},{1,9},{5... | collective-permute-start | bytes 393224 | tf_op jit(solution)/shard_map/ppermute | solution.py:19
  17.0 0.3 collective-permute-done.1.rest_2_
  17.3 2.0 %collective-permute-start.4 = (bf16[512,128]{1,0:T(8,128)(2,1)S(1)}, bf16[512,128]{1,0:T(8,128)(2,1)S(1)}, u32[]{:S(2)}, u32[]{:S(2)}) collective-permute-start(bf16[512,128]{1,0:T(8,128)(2,1)S(1)} %collective-permute-done.3.rest_4_), channel_id=1, source_target_pairs={{0,4},{4,0},{8,12},{12,8},{16,20},{20,16},{24,28},{28,24},{1,5},{5... | collective-permute-start | bytes 393224 | tf_op jit(solution)/shard_map/ppermute | solution.py:19
  19.3 0.0 collective-permute-done.rest_1_
  19.3 0.2 collective-permute-start.9
  19.5 1.0 %collective-permute-done.12.rest_13_ = bf16[512,128]{1,0:T(8,128)(2,1)S(1)} collective-permute-done((bf16[512,128]{1,0:T(8,128)(2,1)S(1)}, bf16[512,128]{1,0:T(8,128)(2,1)S(1)}, u32[]{:S(2)}, u32[]{:S(2)}) %collective-permute-start.12) | collective-permute-done | bytes 131104 | tf_op jit(solution)/shard_map/ppermute | solution.py:19
  20.5 1.7 %collective-permute-start.2 = (bf16[512,128]{1,0:T(8,128)(2,1)S(1)}, bf16[512,128]{1,0:T(8,128)(2,1)S(1)}, u32[]{:S(2)}, u32[]{:S(2)}) collective-permute-start(bf16[512,128]{1,0:T(8,128)(2,1)S(1)} %collective-permute-done.1.rest_2_), channel_id=1, source_target_pairs={{0,4},{4,0},{8,12},{12,8},{16,20},{20,16},{24,28},{28,24},{1,5},{5... | collective-permute-start | bytes 393224 | tf_op jit(solution)/shard_map/ppermute | solution.py:19
  22.1 0.0 collective-permute-done.11.rest_12_
  22.1 0.4 collective-permute-start.13
  22.5 0.0 collective-permute-done.5.rest_6_
  22.5 1.7 %collective-permute-start.6 = (bf16[512,128]{1,0:T(8,128)(2,1)S(1)}, bf16[512,128]{1,0:T(8,128)(2,1)S(1)}, u32[]{:S(2)}, u32[]{:S(2)}) collective-permute-start(bf16[512,128]{1,0:T(8,128)(2,1)S(1)} %collective-permute-done.5.rest_6_), channel_id=1, source_target_pairs={{0,4},{4,0},{8,12},{12,8},{16,20},{20,16},{24,28},{28,24},{1,5},{5... | collective-permute-start | bytes 393224 | tf_op jit(solution)/shard_map/ppermute | solution.py:19
  24.2 2.3 %collective-permute-done.9.rest_10_ = bf16[512,128]{1,0:T(8,128)(2,1)S(1)} collective-permute-done((bf16[512,128]{1,0:T(8,128)(2,1)S(1)}, bf16[512,128]{1,0:T(8,128)(2,1)S(1)}, u32[]{:S(2)}, u32[]{:S(2)}) %collective-permute-start.9) | collective-permute-done | bytes 131104 | tf_op jit(solution)/shard_map/ppermute | solution.py:19
  26.5 0.0 collective-permute-done.4.rest_5_
  26.5 2.8 %collective-permute-done.2.rest_3_ = bf16[512,128]{1,0:T(8,128)(2,1)S(1)} collective-permute-done((bf16[512,128]{1,0:T(8,128)(2,1)S(1)}, bf16[512,128]{1,0:T(8,128)(2,1)S(1)}, u32[]{:S(2)}, u32[]{:S(2)}) %collective-permute-start.2) | collective-permute-done | bytes 131104 | tf_op jit(solution)/shard_map/ppermute | solution.py:19
  29.3 2.8 %collective-permute-done.13.rest_14_ = bf16[512,128]{1,0:T(8,128)(2,1)S(1)} collective-permute-done((bf16[512,128]{1,0:T(8,128)(2,1)S(1)}, bf16[512,128]{1,0:T(8,128)(2,1)S(1)}, u32[]{:S(2)}, u32[]{:S(2)}) %collective-permute-start.13) | collective-permute-done | bytes 131104 | tf_op jit(solution)/shard_map/ppermute | solution.py:19
  32.1 1.6 %collective-permute-done.6.rest_7_ = bf16[512,128]{1,0:T(8,128)(2,1)S(1)} collective-permute-done((bf16[512,128]{1,0:T(8,128)(2,1)S(1)}, bf16[512,128]{1,0:T(8,128)(2,1)S(1)}, u32[]{:S(2)}, u32[]{:S(2)}) %collective-permute-start.6) | collective-permute-done | bytes 131104 | tf_op jit(solution)/shard_map/ppermute | solution.py:19
  33.7 0.0 copy-start
  33.7 2.2 %copy-done = bf16[1024,2048]{1,0:T(8,128)(2,1)S(1)} copy-done((bf16[1024,2048]{1,0:T(8,128)(2,1)S(1)}, bf16[1024,2048]{1,0:T(8,128)(2,1)}, u32[]{:S(2)}) %copy-start) | copy-done | bytes 4194328
  35.9 0.0 copy-start.1
  35.9 1.0 %copy-done.1 = bf16[256,1024]{1,0:T(8,128)(2,1)S(1)} copy-done((bf16[256,1024]{1,0:T(8,128)(2,1)S(1)}, bf16[256,1024]{1,0:T(8,128)(2,1)}, u32[]{:S(2)}) %copy-start.1) | copy-done | bytes 524312
  37.0 0.0 copy-start.2
  37.0 0.9 %copy-done.2 = bf16[256,2,128]{2,1,0:T(2,128)(2,1)S(1)} copy-done((bf16[256,2,128]{2,1,0:T(2,128)(2,1)S(1)}, bf16[256,2,128]{2,1,0:T(2,128)(2,1)}, u32[]{:S(2)}) %copy-start.2) | copy-done | bytes 131096
  37.9 0.0 copy-start.3
  37.9 0.9 %copy-done.3 = bf16[256,2,128]{2,1,0:T(2,128)(2,1)S(1)} copy-done((bf16[256,2,128]{2,1,0:T(2,128)(2,1)S(1)}, bf16[256,2,128]{2,1,0:T(2,128)(2,1)}, u32[]{:S(2)}) %copy-start.3) | copy-done | bytes 131096
  38.8 0.0 copy-start.4
  38.8 0.7 copy-done.4
  39.4 0.0 copy-start.5
  39.4 0.7 copy-done.5
  40.1 0.7 copy-done.6
  40.8 13.5 %attend.1 = (bf16[2,256,512]{2,1,0:T(8,128)(2,1)S(1)}, f32[2,256,512]{2,1,0:T(8,128)S(1)}) custom-call(s32[1,4]{1,0:T(1,128)S(1)} %copy-done.4, s32[1,3]{1,0:T(1,128)S(1)} %copy-done.5, s32[1,3]{1,0:T(1,128)S(1)} %bitcast.13, bf16[256,1024]{1,0:T(8,128)(2,1)S(1)} %copy-done.1, bf16[512,128]{1,0:T(8,128)(2,1)S(1)} %bitcast.8, bf16[1024,2048]{1,0:T(8,128)(2,1)S(1)} %copy-done, ...), custom_call_target="tpu_custom_call" | custom-call | flops 2684354560 | bytes 8388608 | tf_op jit(solution)/shard_map/attend/pallas_call | solution.py:202
  54.2 0.1 collective-permute-start.14
  54.3 1.9 %collective-permute-done.14 = bf16[2,256,512]{2,1,0:T(8,128)(2,1)S(1)} collective-permute-done((bf16[2,256,512]{2,1,0:T(8,128)(2,1)S(1)}, bf16[2,256,512]{2,1,0:T(8,128)(2,1)S(1)}, u32[]{:S(2)}, u32[]{:S(2)}) %collective-permute-start.14) | collective-permute-done | bytes 524320 | tf_op jit(solution)/shard_map/ppermute | solution.py:19
  56.2 0.2 convert_add_fusion
  56.4 1.6 %collective-permute-start.15 = (bf16[1,256,512]{2,1,0:T(8,128)(2,1)S(1)}, bf16[1,256,512]{2,1,0:T(8,128)(2,1)S(1)}, u32[]{:S(2)}, u32[]{:S(2)}) collective-permute-start(bf16[1,256,512]{2,1,0:T(8,128)(2,1)S(1)} %slice.19), channel_id=1, source_target_pairs={{0,2},{1,3},{2,0},{3,1},{4,6},{5,7},{6,4},{7,5},{8,10},{9,11},{10,... | collective-permute-start | bytes 786440 | tf_op jit(solution)/shard_map/ppermute | solution.py:19
  58.0 6.8 %collective-permute-done.15 = bf16[1,256,512]{2,1,0:T(8,128)(2,1)S(1)} collective-permute-done((bf16[1,256,512]{2,1,0:T(8,128)(2,1)S(1)}, bf16[1,256,512]{2,1,0:T(8,128)(2,1)S(1)}, u32[]{:S(2)}, u32[]{:S(2)}) %collective-permute-start.15) | collective-permute-done | bytes 262176 | tf_op jit(solution)/shard_map/ppermute | solution.py:19
  64.8 0.8 %fusion.1 = bf16[256,512]{1,0:T(8,128)(2,1)} fusion(bf16[1,256,512]{2,1,0:T(8,128)(2,1)S(1)} %collective-permute-done.15, f32[2,256,512]{2,1,0:T(8,128)S(1)} %convert_add_fusion), kind=kLoop, calls=%fused_computation.4 | loop fusion | flops 393216 | bytes 1048576 | tf_op jit(solution)/shard_map/convert_element_type | solution.py:246
  (2 shorter events, 0.0 us)
Async XLA Ops:
  0.0 11.9 %collective-permute-start.10 = (bf16[512,128]{1,0:T(8,128)(2,1)}, bf16[512,128]{1,0:T(8,128)(2,1)S(1)}, u32[]{:S(2)}, u32[]{:S(2)}) collective-permute-start(bf16[512,128]{1,0:T(8,128)(2,1)} %bitcast.5), channel_id=1, source_target_pairs={{0,16},{4,20},{8,24},{12,28},{16,0},{20,4},{24,8},{28,12},{1,17},{... | collective-permute-start | bytes 393224 | tf_op jit(solution)/shard_map/ppermute | solution.py:19
  4.1 10.3 %collective-permute-start.8 = (bf16[512,128]{1,0:T(8,128)(2,1)}, bf16[512,128]{1,0:T(8,128)(2,1)S(1)}, u32[]{:S(2)}, u32[]{:S(2)}) collective-permute-start(bf16[512,128]{1,0:T(8,128)(2,1)} %bitcast.6), channel_id=1, source_target_pairs={{0,8},{4,12},{8,0},{12,4},{16,24},{20,28},{24,16},{28,20},{1,9},{5... | collective-permute-start | bytes 393224 | tf_op jit(solution)/shard_map/ppermute | solution.py:19
  5.6 8.7 %collective-permute-start.7 = (bf16[512,128]{1,0:T(8,128)(2,1)}, bf16[512,128]{1,0:T(8,128)(2,1)S(1)}, u32[]{:S(2)}, u32[]{:S(2)}) collective-permute-start(bf16[512,128]{1,0:T(8,128)(2,1)} %bitcast.7), channel_id=1, source_target_pairs={{0,4},{4,0},{8,12},{12,8},{16,20},{20,16},{24,28},{28,24},{1,5},{5... | collective-permute-start | bytes 393224 | tf_op jit(solution)/shard_map/ppermute | solution.py:19
  7.1 9.2 %collective-permute-start.3 = (bf16[512,128]{1,0:T(8,128)(2,1)}, bf16[512,128]{1,0:T(8,128)(2,1)S(1)}, u32[]{:S(2)}, u32[]{:S(2)}) collective-permute-start(bf16[512,128]{1,0:T(8,128)(2,1)} %bitcast.9), channel_id=1, source_target_pairs={{0,16},{4,20},{8,24},{12,28},{16,0},{20,4},{24,8},{28,12},{1,17},{... | collective-permute-start | bytes 393224 | tf_op jit(solution)/shard_map/ppermute | solution.py:19
  7.5 9.8 %collective-permute-start.1 = (bf16[512,128]{1,0:T(8,128)(2,1)}, bf16[512,128]{1,0:T(8,128)(2,1)S(1)}, u32[]{:S(2)}, u32[]{:S(2)}) collective-permute-start(bf16[512,128]{1,0:T(8,128)(2,1)} %bitcast.10), channel_id=1, source_target_pairs={{0,8},{4,12},{8,0},{12,4},{16,24},{20,28},{24,16},{28,20},{1,9},{5... | collective-permute-start | bytes 393224 | tf_op jit(solution)/shard_map/ppermute | solution.py:19
  11.9 7.4 %collective-permute-start = (bf16[512,128]{1,0:T(8,128)(2,1)}, bf16[512,128]{1,0:T(8,128)(2,1)S(1)}, u32[]{:S(2)}, u32[]{:S(2)}) collective-permute-start(bf16[512,128]{1,0:T(8,128)(2,1)} %bitcast.11), channel_id=1, source_target_pairs={{0,4},{4,0},{8,12},{12,8},{16,20},{20,16},{24,28},{28,24},{1,5},{5... | collective-permute-start | bytes 393224 | tf_op jit(solution)/shard_map/ppermute | solution.py:19
  14.3 6.1 %collective-permute-start.12 = (bf16[512,128]{1,0:T(8,128)(2,1)S(1)}, bf16[512,128]{1,0:T(8,128)(2,1)S(1)}, u32[]{:S(2)}, u32[]{:S(2)}) collective-permute-start(bf16[512,128]{1,0:T(8,128)(2,1)S(1)} %collective-permute-done.10.rest_11_), channel_id=1, source_target_pairs={{0,8},{4,12},{8,0},{12,4},{16,24},{20,28},{24,16},{28,20},{1,9},{5... | collective-permute-start | bytes 393224 | tf_op jit(solution)/shard_map/ppermute | solution.py:19
  14.3 7.8 %collective-permute-start.11 = (bf16[512,128]{1,0:T(8,128)(2,1)S(1)}, bf16[512,128]{1,0:T(8,128)(2,1)S(1)}, u32[]{:S(2)}, u32[]{:S(2)}) collective-permute-start(bf16[512,128]{1,0:T(8,128)(2,1)S(1)} %collective-permute-done.10.rest_11_), channel_id=1, source_target_pairs={{0,4},{4,0},{8,12},{12,8},{16,20},{20,16},{24,28},{28,24},{1,5},{5... | collective-permute-start | bytes 393224 | tf_op jit(solution)/shard_map/ppermute | solution.py:19
  16.3 6.2 %collective-permute-start.5 = (bf16[512,128]{1,0:T(8,128)(2,1)S(1)}, bf16[512,128]{1,0:T(8,128)(2,1)S(1)}, u32[]{:S(2)}, u32[]{:S(2)}) collective-permute-start(bf16[512,128]{1,0:T(8,128)(2,1)S(1)} %collective-permute-done.3.rest_4_), channel_id=1, source_target_pairs={{0,8},{4,12},{8,0},{12,4},{16,24},{20,28},{24,16},{28,20},{1,9},{5... | collective-permute-start | bytes 393224 | tf_op jit(solution)/shard_map/ppermute | solution.py:19
  17.3 9.2 %collective-permute-start.4 = (bf16[512,128]{1,0:T(8,128)(2,1)S(1)}, bf16[512,128]{1,0:T(8,128)(2,1)S(1)}, u32[]{:S(2)}, u32[]{:S(2)}) collective-permute-start(bf16[512,128]{1,0:T(8,128)(2,1)S(1)} %collective-permute-done.3.rest_4_), channel_id=1, source_target_pairs={{0,4},{4,0},{8,12},{12,8},{16,20},{20,16},{24,28},{28,24},{1,5},{5... | collective-permute-start | bytes 393224 | tf_op jit(solution)/shard_map/ppermute | solution.py:19
  19.3 7.2 %collective-permute-start.9 = (bf16[512,128]{1,0:T(8,128)(2,1)S(1)}, bf16[512,128]{1,0:T(8,128)(2,1)S(1)}, u32[]{:S(2)}, u32[]{:S(2)}) collective-permute-start(bf16[512,128]{1,0:T(8,128)(2,1)S(1)} %collective-permute-done.8.rest_9_), channel_id=1, source_target_pairs={{0,4},{4,0},{8,12},{12,8},{16,20},{20,16},{24,28},{28,24},{1,5},{5... | collective-permute-start | bytes 393224 | tf_op jit(solution)/shard_map/ppermute | solution.py:19
  20.5 8.8 %collective-permute-start.2 = (bf16[512,128]{1,0:T(8,128)(2,1)S(1)}, bf16[512,128]{1,0:T(8,128)(2,1)S(1)}, u32[]{:S(2)}, u32[]{:S(2)}) collective-permute-start(bf16[512,128]{1,0:T(8,128)(2,1)S(1)} %collective-permute-done.1.rest_2_), channel_id=1, source_target_pairs={{0,4},{4,0},{8,12},{12,8},{16,20},{20,16},{24,28},{28,24},{1,5},{5... | collective-permute-start | bytes 393224 | tf_op jit(solution)/shard_map/ppermute | solution.py:19
  22.1 10.0 %collective-permute-start.13 = (bf16[512,128]{1,0:T(8,128)(2,1)S(1)}, bf16[512,128]{1,0:T(8,128)(2,1)S(1)}, u32[]{:S(2)}, u32[]{:S(2)}) collective-permute-start(bf16[512,128]{1,0:T(8,128)(2,1)S(1)} %collective-permute-done.12.rest_13_), channel_id=1, source_target_pairs={{0,4},{4,0},{8,12},{12,8},{16,20},{20,16},{24,28},{28,24},{1,5},{5... | collective-permute-start | bytes 393224 | tf_op jit(solution)/shard_map/ppermute | solution.py:19
  22.5 11.2 %collective-permute-start.6 = (bf16[512,128]{1,0:T(8,128)(2,1)S(1)}, bf16[512,128]{1,0:T(8,128)(2,1)S(1)}, u32[]{:S(2)}, u32[]{:S(2)}) collective-permute-start(bf16[512,128]{1,0:T(8,128)(2,1)S(1)} %collective-permute-done.5.rest_6_), channel_id=1, source_target_pairs={{0,4},{4,0},{8,12},{12,8},{16,20},{20,16},{24,28},{28,24},{1,5},{5... | collective-permute-start | bytes 393224 | tf_op jit(solution)/shard_map/ppermute | solution.py:19
  33.7 2.2 %copy-start = (bf16[1024,2048]{1,0:T(8,128)(2,1)S(1)}, bf16[1024,2048]{1,0:T(8,128)(2,1)}, u32[]{:S(2)}) copy-start(bf16[1024,2048]{1,0:T(8,128)(2,1)} %proj_ref.1) | copy-start | bytes 12582916
  35.9 1.0 %copy-start.1 = (bf16[256,1024]{1,0:T(8,128)(2,1)S(1)}, bf16[256,1024]{1,0:T(8,128)(2,1)}, u32[]{:S(2)}) copy-start(bf16[256,1024]{1,0:T(8,128)(2,1)} %query_ref.1) | copy-start | bytes 1572868
  37.0 0.9 %copy-start.2 = (bf16[256,2,128]{2,1,0:T(2,128)(2,1)S(1)}, bf16[256,2,128]{2,1,0:T(2,128)(2,1)}, u32[]{:S(2)}) copy-start(bf16[256,2,128]{2,1,0:T(2,128)(2,1)} %param.8) | copy-start | bytes 393220
  37.9 0.9 %copy-start.3 = (bf16[256,2,128]{2,1,0:T(2,128)(2,1)S(1)}, bf16[256,2,128]{2,1,0:T(2,128)(2,1)}, u32[]{:S(2)}) copy-start(bf16[256,2,128]{2,1,0:T(2,128)(2,1)} %param.9) | copy-start | bytes 393220
  38.8 0.7 copy-start.4
  39.4 0.7 copy-start.5
  40.1 0.7 copy-start.6
  54.2 2.0 %collective-permute-start.14 = (bf16[2,256,512]{2,1,0:T(8,128)(2,1)S(1)}, bf16[2,256,512]{2,1,0:T(8,128)(2,1)S(1)}, u32[]{:S(2)}, u32[]{:S(2)}) collective-permute-start(bf16[2,256,512]{2,1,0:T(8,128)(2,1)S(1)} %get-tuple-element.8), channel_id=1, source_target_pairs={{0,1},{1,0},{2,3},{3,2},{4,5},{5,4},{6,7},{7,6},{8,9},{9,8},{10,11... | collective-permute-start | bytes 1572872 | tf_op jit(solution)/shard_map/ppermute | solution.py:19
  56.4 8.4 %collective-permute-start.15 = (bf16[1,256,512]{2,1,0:T(8,128)(2,1)S(1)}, bf16[1,256,512]{2,1,0:T(8,128)(2,1)S(1)}, u32[]{:S(2)}, u32[]{:S(2)}) collective-permute-start(bf16[1,256,512]{2,1,0:T(8,128)(2,1)S(1)} %slice.19), channel_id=1, source_target_pairs={{0,2},{1,3},{2,0},{3,1},{4,6},{5,7},{6,4},{7,5},{8,10},{9,11},{10,... | collective-permute-start | bytes 786440 | tf_op jit(solution)/shard_map/ppermute | solution.py:19

commit v2 on v1

v2 whole, which is shorter than its diff:
```python
import functools
import math

import jax
import jax.numpy as jnp
from jax import lax
from jax.experimental import pallas as pl
from jax.experimental.pallas import tpu as pltpu
from jax.sharding import PartitionSpec as P

PAGE = 128
LANES = 128
FAR = 1e30
TREE_MAX = 16


def swapped(value, axis, mask):
    count = lax.axis_size(axis)
    return lax.ppermute(value, axis, [(source, source ^ mask) for source in range(count)])


def passed_along(value, axis, steps):
    count = lax.axis_size(axis)
    return lax.ppermute(value, axis, [(source, (source + steps) % count) for source in range(count)])


def gathered(own, axis):
    blocks = {0: own}
    for mask in range(1, lax.axis_size(axis)):
        low = mask & -mask
        blocks[mask] = swapped(blocks[mask - low], axis, low)
    return [blocks[mask] for mask in range(len(blocks))]


def rotate(value, amount, shards):
    reduced = amount % shards
    for bit_number in range(max(1, (shards - 1).bit_length())):
        moved = passed_along(value, "seq", 1 << bit_number)
        value = jnp.where(reduced // (1 << bit_number) % 2 == 1, moved, value)
    return value


def planar(source, wide, count):
    wide[pl.ds(0, 2 * count), :] = source[...].astype(jnp.float32)
    return (
        wide[pl.ds(0, count, stride=2), :].astype(jnp.bfloat16),
        wide[pl.ds(1, count, stride=2), :].astype(jnp.bfloat16),
    )


def stage_kernel(sizes, page_ref, shift_ref, live_ref, query_in, own_in, proj_in, *rest):
    table, query_out, proj_out, keys_out, values_out, raw, wide, sems = rest
    own_copy = pltpu.make_async_copy(own_in, raw, sems.at[0])
    query_copy = pltpu.make_async_copy(query_in, query_out, sems.at[1])
    proj_copy = pltpu.make_async_copy(proj_in, proj_out, sems.at[2])
    own_copy.start()
    query_copy.start()
    proj_copy.start()
    shards, per_shard = sizes["shards"], sizes["per_shard"]
    me = lax.axis_index("seq")
    seen = []
    for k in range(sizes["slash_count"]):
        distance = shift_ref[0, k]
        older = distance > me
        source = jnp.where(older, shards + me - distance, me - distance)
        live = live_ref[0, k] == 1
        seen.append((live & older, source))
        choice = (source ^ me) + jnp.where(older, 0, shards)
        table[0, 2 * k] = choice
        table[0, 2 * k + 1] = live.astype(jnp.int32)
    for i in range(sizes["page_count"]):
        page = page_ref[0, i]
        owner = page // per_shard
        clash = functools.reduce(
            jnp.logical_or, [active & (source == owner) for active, source in seen]
        )
        base = 2 * sizes["slash_count"] + 3 * i
        table[0, base] = owner ^ me
        table[0, base + 1] = page - owner * per_shard
        table[0, base + 2] = jnp.logical_not(clash).astype(jnp.int32)
    own_copy.wait()
    count = keys_out.shape[0]
    own_keys, own_values = planar(raw, wide, count)
    keys_out[...] = own_keys
    values_out[:, pl.ds(0, own_values.shape[1])] = own_values
    values_out[:, pl.ds(own_values.shape[1], LANES)] = jnp.ones((count, LANES), jnp.bfloat16)
    query_copy.wait()
    proj_copy.wait()


def attention_kernel(sizes, table, query_ref, proj_ref, own_keys, own_values, *rest):
    shards, heads, head_width = sizes["shards"], sizes["heads"], sizes["head_width"]
    slash_count, page_count = sizes["slash_count"], sizes["page_count"]
    page_rows, members, tree = sizes["page_rows"], sizes["members"], sizes["tree"]
    store_count = (2 * shards - 1) if tree else (slash_count + page_count)
    stores = rest[:store_count]
    send_ref, keep_ref = rest[store_count : store_count + 2]
    raw, wide, keys, values, scores, weights, attended, sems = rest[store_count + 2 :]
    rows = query_ref.shape[0]

    def slot(number):
        if number < slash_count:
            return raw.at[pl.ds(number * 2 * rows, 2 * rows)]
        first = slash_count * 2 * rows + (number - slash_count) * 2 * page_rows
        return raw.at[pl.ds(first, 2 * page_rows)]

    for k in range(slash_count):
        if not tree:
            pltpu.make_async_copy(stores[k], slot(k), sems.at[k]).start()
            continue
        for choice in range(2 * shards):
            if choice == shards:
                continue
            source = stores[choice] if choice < shards else stores[choice - 1]

            @pl.when(table[0, 2 * k] == choice)
            def _(source=source):
                pltpu.make_async_copy(source, slot(k), sems.at[k]).start()

    for i in range(page_count):
        number = slash_count + i
        base = 2 * slash_count + 3 * i
        if not tree:
            pltpu.make_async_copy(stores[number], slot(number), sems.at[number]).start()
            continue
        first = pl.multiple_of(table[0, base + 1] * (2 * page_rows), 2 * page_rows)
        for mask in range(shards):

            @pl.when(table[0, base] == mask)
            def _(mask=mask):
                pltpu.make_async_copy(
                    stores[mask].at[pl.ds(first, 2 * page_rows)], slot(number), sems.at[number]
                ).start()

    keys[pl.ds(0, rows), :] = own_keys[...]
    values[pl.ds(0, rows), :] = own_values[...]
    chunks = [(0, rows, None)]
    first = rows
    values[pl.ds(rows, values.shape[0] - rows), pl.ds(head_width, LANES)] = jnp.ones(
        (values.shape[0] - rows, LANES), jnp.bfloat16
    )
    for number in range(slash_count + page_count):
        count = rows if number < slash_count else page_rows
        place = slot(number)
        pltpu.make_async_copy(place, place, sems.at[number]).wait()
        new_keys, new_values = planar(place, wide.at[pl.ds(2 * first, 2 * count)], count)
        keys[pl.ds(first, count), :] = new_keys
        values[pl.ds(first, count), pl.ds(0, head_width)] = new_values
        at = 2 * number + 1 if number < slash_count else 2 * slash_count + 3 * (number - slash_count) + 2
        chunks.append((first, count, table[0, at] == 1))
        first += count
    scale = head_width**-0.5 * math.log2(math.e)
    causal = lax.broadcasted_iota(jnp.int32, (rows, rows), 0) >= lax.broadcasted_iota(
        jnp.int32, (rows, rows), 1
    )

    def score(head, chunk, highest):
        start, count, flag = chunk
        part = lax.dot_general(
            query_ref[:, pl.ds(head * head_width, head_width)],
            keys[pl.ds(start, count), :],
            (((1,), (1,)), ((), ())),
            preferred_element_type=jnp.float32,
        )
        if flag is None:
            part = jnp.where(causal, part, -FAR)
        scores[head % 2, :, pl.ds(start, count)] = part
        top = functools.reduce(
            jnp.maximum, [part[:, at : at + LANES] for at in range(0, count, LANES)]
        )
        if flag is not None:
            top = jnp.where(flag, top, -FAR)
        return top if highest is None else jnp.maximum(highest, top)

    def weigh(head, chunk, highest):
        start, count, flag = chunk
        level = highest if flag is None else jnp.where(flag, highest, FAR)
        part = jnp.exp2((scores[head % 2, :, pl.ds(start, count)] - level) * scale)
        weights[head % 2, :, pl.ds(start, count)] = part.astype(jnp.bfloat16)

    running = None
    for chunk in chunks:
        running = score(0, chunk, running)
    for head in range(heads):
        highest = jnp.max(running, axis=1, keepdims=True)
        running = None
        for chunk in chunks:
            if head + 1 < heads:
                running = score(head + 1, chunk, running)
            weigh(head, chunk, highest)
        total = jnp.dot(weights[head % 2], values[...], preferred_element_type=jnp.float32)
        attended[:, pl.ds(head * head_width, head_width)] = (
            total[:, :head_width] / total[:, head_width:]
        ).astype(jnp.bfloat16)

    mine = lax.axis_index("head")
    block = proj_ref.shape[1] // members
    for mask in range(members):
        column = pl.multiple_of((mine ^ mask) * block, block)
        term = jnp.dot(
            attended[...], proj_ref[:, pl.ds(column, block)], preferred_element_type=jnp.float32
        )
        if mask % 2:
            send_ref[mask // 2] = term.astype(send_ref.dtype)
        else:
            keep_ref[mask // 2] = term


def body(queries, keys_values, cache_kv, vertical_pages, slash_shift, slash_live, out_proj):
    row_count = queries.shape[0]
    head_width = keys_values.shape[2]
    heads = queries.shape[1] // head_width
    shards = lax.axis_size("seq")
    members = lax.axis_size("head")
    slash_count = slash_shift.shape[1]
    page_count = vertical_pages.shape[1]
    per_shard = row_count // PAGE
    out_width = out_proj.shape[1]
    own = keys_values.reshape(2 * row_count, head_width)
    tree = shards <= TREE_MAX and shards & (shards - 1) == 0
    if tree:
        cache = cache_kv.reshape(2 * row_count, head_width)
        stores = gathered(cache, "seq") + gathered(own, "seq")[1:]
    else:
        own_shard = lax.axis_index("seq")
        stores = []
        for k in range(slash_count):
            distance = slash_shift[0, k]
            payload = jnp.where(own_shard < shards - distance, keys_values, cache_kv)
            stores.append(rotate(payload, distance, shards).reshape(2 * row_count, head_width))
        whole = lax.all_gather(cache_kv, "seq", axis=0, tiled=True)
        for i in range(page_count):
            page = lax.dynamic_slice_in_dim(whole, vertical_pages[0, i] * PAGE, PAGE, 0)
            stores.append(page.reshape(2 * PAGE, head_width))
    key_count = (1 + slash_count) * row_count + page_count * PAGE
    sizes = dict(
        shards=shards, heads=heads, head_width=head_width, slash_count=slash_count,
        page_count=page_count, page_rows=PAGE, per_shard=per_shard, members=members, tree=tree,
    )
    hbm = pl.BlockSpec(memory_space=pltpu.HBM)
    scalars = pl.BlockSpec(memory_space=pltpu.SMEM)
    vector = pl.BlockSpec(memory_space=pltpu.VMEM)
    block = out_width // members
    table, query_near, proj_near, own_keys, own_values = pl.pallas_call(
        functools.partial(stage_kernel, sizes),
        out_shape=[
            jax.ShapeDtypeStruct((1, 2 * slash_count + 3 * page_count), jnp.int32),
            jax.ShapeDtypeStruct(queries.shape, queries.dtype),
            jax.ShapeDtypeStruct(out_proj.shape, out_proj.dtype),
            jax.ShapeDtypeStruct((row_count, head_width), jnp.bfloat16),
            jax.ShapeDtypeStruct((row_count, head_width + LANES), jnp.bfloat16),
        ],
        in_specs=[scalars] * 3 + [hbm] * 3,
        out_specs=[scalars] + [vector] * 4,
        scratch_shapes=[
            pltpu.VMEM((2 * row_count, head_width), jnp.bfloat16),
            pltpu.VMEM((2 * row_count, head_width), jnp.float32),
            pltpu.SemaphoreType.DMA((3,)),
        ],
        compiler_params=pltpu.CompilerParams(vmem_limit_bytes=8 << 20),
        cost_estimate=pl.CostEstimate(flops=0, bytes_accessed=10 << 20, transcendentals=0),
        name="stage",
    )(
        vertical_pages,
        slash_shift,
        slash_live.reshape(1, slash_count),
        queries,
        own,
        out_proj,
    )
    send, keep = pl.pallas_call(
        functools.partial(attention_kernel, sizes),
        out_shape=[
            jax.ShapeDtypeStruct((members // 2, row_count, block), jnp.bfloat16),
            jax.ShapeDtypeStruct((members // 2, row_count, block), jnp.float32),
        ],
        in_specs=[scalars] + [vector] * (4 + len(stores)),
        out_specs=[vector, vector],
        scratch_shapes=[
            pltpu.VMEM((2 * (key_count - row_count), head_width), jnp.bfloat16),
            pltpu.VMEM((2 * key_count, head_width), jnp.float32),
            pltpu.VMEM((key_count, head_width), jnp.bfloat16),
            pltpu.VMEM((key_count, head_width + LANES), jnp.bfloat16),
            pltpu.VMEM((2, row_count, key_count), jnp.float32),
            pltpu.VMEM((2, row_count, key_count), jnp.bfloat16),
            pltpu.VMEM((row_count, heads * head_width), jnp.bfloat16),
            pltpu.SemaphoreType.DMA((slash_count + page_count,)),
        ],
        compiler_params=pltpu.CompilerParams(vmem_limit_bytes=32 << 20),
        cost_estimate=pl.CostEstimate(
            flops=4 * heads * row_count * key_count * head_width
            + 2 * row_count * heads * head_width * out_width,
            bytes_accessed=8 << 20,
            transcendentals=heads * row_count * key_count,
        ),
        name="attend",
    )(table, query_near, proj_near, own_keys, own_values, *stores)
    step = 1
    while step < members:
        keep = keep + swapped(send, "head", step).astype(jnp.float32)
        step *= 2
        if step < members:
            send = keep[1::2].astype(jnp.bfloat16)
            keep = keep[0::2]
    return keep[0].astype(jnp.bfloat16)


def solution(mesh):
    placed = (
        P("seq", "head"),
        P("seq", None, "head"),
        P("seq", None, "head"),
        P("head", None),
        P("head", None),
        P("seq", "head", None),
        P("head", None),
    )
    return jax.shard_map(
        body, mesh=mesh, in_specs=placed, out_specs=P("seq", "head"), check_vma=False
    )
```

time: 65.9 us -> 54.2 us (0.82)
  waiting for transfers between devices: 24.8 us -> 17 us
  Pallas kernels: 13.5 us -> 10.6 us
  local copies, waits for them, and re-layouts: 7.03 us -> 6.13 us
    ppermute x16, waiting for transfers between devices: 24.8 us -> 17 us  [swapped(): lax.ppermute(value, axis, [(source, source ^ mask) for source in range(co...]
    pallas_call x1, Pallas kernels: 13.5 us -> 8.87 us  [body(): pl.pallas_call(functools.partial(attention_kernel, sizes), out_shape=[jax...]
    pallas_call x0 -> x1, Pallas kernels: none -> 1.77 us  [body(): pl.pallas_call(functools.partial(stage_kernel, sizes), out_shape=[jax.Sha...]
    unnamed x14, local copies, waits for them, and re-layouts: 7 us -> 6.1 us
  transfers between devices with their start and end apart: 16 -> 16, of which waited for: 10 -> 7; matrix products, arithmetic and copies ran while one was open for 0% -> 0% of each run, Pallas kernels for 0% -> 3%
where the time goes in v2:
time: 54.2 us; the launch traced here: 54 us
  starting transfers between devices  19.2 us (35%)
  waiting for transfers between devices  17 us (31%)
  Pallas kernels  10.6 us (20%)
  local copies, waits for them, and re-layouts  6.13 us (11%)
  other arithmetic  0.95 us (2%)
    ppermute x16, starting transfers between devices, swapped(): lax.ppermute(value, axis, [(source, source ^ mask) for source in range(co...  19.2 us
    ppermute x16, waiting for transfers between devices, swapped(): lax.ppermute(value, axis, [(source, source ^ mask) for source in range(co...  17 us
    pallas_call x1, Pallas kernels, body(): pl.pallas_call(functools.partial(attention_kernel, sizes), out_shape=[jax...  8.87 us
    unnamed x14, local copies, waits for them, and re-layouts  6.1 us
    pallas_call x1, Pallas kernels, body(): pl.pallas_call(functools.partial(stage_kernel, sizes), out_shape=[jax.Sha...  1.77 us
  transfers between devices with their start and end apart: 16, of which 7 were waited for; matrix products, arithmetic and copies ran while one was open for 0% of the time, Pallas kernels for 3%

profile of v2, /device:TPU:0, one launch (start us, length us, event | category | flops | bytes accessed | tf_op | source)
XLA Modules:
  0.0 54.0 jit_solution(13336147747870012325)
XLA Ops:
  0.0 4.1 %collective-permute-start.10 = (bf16[512,128]{1,0:T(8,128)(2,1)}, bf16[512,128]{1,0:T(8,128)(2,1)S(1)}, u32[]{:S(2)}, u32[]{:S(2)}) collective-permute-start(bf16[512,128]{1,0:T(8,128)(2,1)} %bitcast.5), channel_id=1, source_target_pairs={{0,16},{4,20},{8,24},{12,28},{16,0},{20,4},{24,8},{28,12},{1,17},{... | collective-permute-start | bytes 393224 | tf_op jit(solution)/shard_map/ppermute | solution.py:19
  4.1 1.6 %collective-permute-start.8 = (bf16[512,128]{1,0:T(8,128)(2,1)}, bf16[512,128]{1,0:T(8,128)(2,1)S(1)}, u32[]{:S(2)}, u32[]{:S(2)}) collective-permute-start(bf16[512,128]{1,0:T(8,128)(2,1)} %bitcast.6), channel_id=1, source_target_pairs={{0,8},{4,12},{8,0},{12,4},{16,24},{20,28},{24,16},{28,20},{1,9},{5... | collective-permute-start | bytes 393224 | tf_op jit(solution)/shard_map/ppermute | solution.py:19
  5.6 1.5 %collective-permute-start.7 = (bf16[512,128]{1,0:T(8,128)(2,1)}, bf16[512,128]{1,0:T(8,128)(2,1)S(1)}, u32[]{:S(2)}, u32[]{:S(2)}) collective-permute-start(bf16[512,128]{1,0:T(8,128)(2,1)} %bitcast.7), channel_id=1, source_target_pairs={{0,4},{4,0},{8,12},{12,8},{16,20},{20,16},{24,28},{28,24},{1,5},{5... | collective-permute-start | bytes 393224 | tf_op jit(solution)/shard_map/ppermute | solution.py:19
  7.1 0.3 collective-permute-start.3
  7.5 0.4 collective-permute-start.1
  7.9 4.0 %collective-permute-done.10.rest_11_ = bf16[512,128]{1,0:T(8,128)(2,1)S(1)} collective-permute-done((bf16[512,128]{1,0:T(8,128)(2,1)}, bf16[512,128]{1,0:T(8,128)(2,1)S(1)}, u32[]{:S(2)}, u32[]{:S(2)}) %collective-permute-start.10) | collective-permute-done | bytes 131104 | tf_op jit(solution)/shard_map/ppermute | solution.py:19
  11.9 2.4 %collective-permute-start = (bf16[512,128]{1,0:T(8,128)(2,1)}, bf16[512,128]{1,0:T(8,128)(2,1)S(1)}, u32[]{:S(2)}, u32[]{:S(2)}) collective-permute-start(bf16[512,128]{1,0:T(8,128)(2,1)} %bitcast.12), channel_id=1, source_target_pairs={{0,4},{4,0},{8,12},{12,8},{16,20},{20,16},{24,28},{28,24},{1,5},{5... | collective-permute-start | bytes 393224 | tf_op jit(solution)/shard_map/ppermute | solution.py:19
  14.3 0.0 collective-permute-done.8.rest_9_
  14.3 0.0 collective-permute-start.12
  14.3 0.0 collective-permute-done.7.rest_8_
  14.3 0.6 %collective-permute-start.11 = (bf16[512,128]{1,0:T(8,128)(2,1)S(1)}, bf16[512,128]{1,0:T(8,128)(2,1)S(1)}, u32[]{:S(2)}, u32[]{:S(2)}) collective-permute-start(bf16[512,128]{1,0:T(8,128)(2,1)S(1)} %collective-permute-done.10.rest_11_), channel_id=1, source_target_pairs={{0,4},{4,0},{8,12},{12,8},{16,20},{20,16},{24,28},{28,24},{1,5},{5... | collective-permute-start | bytes 393224 | tf_op jit(solution)/shard_map/ppermute | solution.py:19
  15.0 1.3 %collective-permute-done.3.rest_4_ = bf16[512,128]{1,0:T(8,128)(2,1)S(1)} collective-permute-done((bf16[512,128]{1,0:T(8,128)(2,1)}, bf16[512,128]{1,0:T(8,128)(2,1)S(1)}, u32[]{:S(2)}, u32[]{:S(2)}) %collective-permute-start.3) | collective-permute-done | bytes 131104 | tf_op jit(solution)/shard_map/ppermute | solution.py:19
  16.3 0.7 %collective-permute-start.5 = (bf16[512,128]{1,0:T(8,128)(2,1)S(1)}, bf16[512,128]{1,0:T(8,128)(2,1)S(1)}, u32[]{:S(2)}, u32[]{:S(2)}) collective-permute-start(bf16[512,128]{1,0:T(8,128)(2,1)S(1)} %collective-permute-done.3.rest_4_), channel_id=1, source_target_pairs={{0,8},{4,12},{8,0},{12,4},{16,24},{20,28},{24,16},{28,20},{1,9},{5... | collective-permute-start | bytes 393224 | tf_op jit(solution)/shard_map/ppermute | solution.py:19
  17.0 0.3 collective-permute-done.1.rest_2_
  17.3 2.0 %collective-permute-start.4 = (bf16[512,128]{1,0:T(8,128)(2,1)S(1)}, bf16[512,128]{1,0:T(8,128)(2,1)S(1)}, u32[]{:S(2)}, u32[]{:S(2)}) collective-permute-start(bf16[512,128]{1,0:T(8,128)(2,1)S(1)} %collective-permute-done.3.rest_4_), channel_id=1, source_target_pairs={{0,4},{4,0},{8,12},{12,8},{16,20},{20,16},{24,28},{28,24},{1,5},{5... | collective-permute-start | bytes 393224 | tf_op jit(solution)/shard_map/ppermute | solution.py:19
  19.3 0.0 collective-permute-done.rest_1_
  19.3 0.2 collective-permute-start.9
  19.5 1.0 %collective-permute-done.12.rest_13_ = bf16[512,128]{1,0:T(8,128)(2,1)S(1)} collective-permute-done((bf16[512,128]{1,0:T(8,128)(2,1)S(1)}, bf16[512,128]{1,0:T(8,128)(2,1)S(1)}, u32[]{:S(2)}, u32[]{:S(2)}) %collective-permute-start.12) | collective-permute-done | bytes 131104 | tf_op jit(solution)/shard_map/ppermute | solution.py:19
  20.5 1.7 %collective-permute-start.2 = (bf16[512,128]{1,0:T(8,128)(2,1)S(1)}, bf16[512,128]{1,0:T(8,128)(2,1)S(1)}, u32[]{:S(2)}, u32[]{:S(2)}) collective-permute-start(bf16[512,128]{1,0:T(8,128)(2,1)S(1)} %collective-permute-done.1.rest_2_), channel_id=1, source_target_pairs={{0,4},{4,0},{8,12},{12,8},{16,20},{20,16},{24,28},{28,24},{1,5},{5... | collective-permute-start | bytes 393224 | tf_op jit(solution)/shard_map/ppermute | solution.py:19
  22.1 0.0 collective-permute-done.11.rest_12_
  22.1 0.4 collective-permute-start.13
  22.5 0.0 collective-permute-done.5.rest_6_
  22.5 1.7 %collective-permute-start.6 = (bf16[512,128]{1,0:T(8,128)(2,1)S(1)}, bf16[512,128]{1,0:T(8,128)(2,1)S(1)}, u32[]{:S(2)}, u32[]{:S(2)}) collective-permute-start(bf16[512,128]{1,0:T(8,128)(2,1)S(1)} %collective-permute-done.5.rest_6_), channel_id=1, source_target_pairs={{0,4},{4,0},{8,12},{12,8},{16,20},{20,16},{24,28},{28,24},{1,5},{5... | collective-permute-start | bytes 393224 | tf_op jit(solution)/shard_map/ppermute | solution.py:19
  24.2 0.0 copy-start
  24.2 2.2 %copy-done = bf16[1024,2048]{1,0:T(8,128)(2,1)S(1)} copy-done((bf16[1024,2048]{1,0:T(8,128)(2,1)S(1)}, bf16[1024,2048]{1,0:T(8,128)(2,1)}, u32[]{:S(2)}) %copy-start) | copy-done | bytes 4194328
  26.4 0.0 copy-start.1
  26.4 1.0 %copy-done.1 = bf16[256,1024]{1,0:T(8,128)(2,1)S(1)} copy-done((bf16[256,1024]{1,0:T(8,128)(2,1)S(1)}, bf16[256,1024]{1,0:T(8,128)(2,1)}, u32[]{:S(2)}) %copy-start.1) | copy-done | bytes 524312
  27.4 0.0 copy-start.2
  27.4 0.9 %copy-done.2 = bf16[256,2,128]{2,1,0:T(2,128)(2,1)S(1)} copy-done((bf16[256,2,128]{2,1,0:T(2,128)(2,1)S(1)}, bf16[256,2,128]{2,1,0:T(2,128)(2,1)}, u32[]{:S(2)}) %copy-start.2) | copy-done | bytes 131096
  28.3 0.0 copy-start.3
  28.3 0.7 %copy-done.3 = s32[1,4]{1,0:T(1,128)S(1)} copy-done((s32[1,4]{1,0:T(1,128)S(1)}, s32[1,4]{1,0:T(1,128)}, u32[]{:S(2)}) %copy-start.3) | copy-done | bytes 40
  29.0 0.0 copy-start.4
  29.0 0.7 %copy-done.4 = s32[1,3]{1,0:T(1,128)S(1)} copy-done((s32[1,3]{1,0:T(1,128)S(1)}, s32[1,3]{1,0:T(1,128)}, u32[]{:S(2)}) %copy-start.4) | copy-done | bytes 36
  29.6 0.7 %copy-done.5 = s32[1,1,3]{2,1,0:T(1,128)S(1)} copy-done((s32[1,1,3]{2,1,0:T(1,128)S(1)}, s32[1,1,3]{2,1,0:T(1,128)}, u32[]{:S(2)}) %copy-start.5) | copy-done | bytes 36
  30.3 1.8 %stage.1 = (s32[1,18]{1,0:T(1,128)S(1)}, bf16[256,1024]{1,0:T(8,128)(2,1)S(1)}, bf16[1024,2048]{1,0:T(8,128)(2,1)S(1)}, bf16[256,128]{1,0:T(8,128)(2,1)S(1)}, bf16[256,256]{1,0:T(8,128)(2,1)S(1)}) custom-call(s32[1,4]{1,0:T(1,128)S(1)} %copy-done.3, s32[1,3]{1,0:T(1,128)S(1)} %copy-done.4, s32[1,3]{1,0:T(1,128)S(1)} %bitcast.9, ...), custom_call_target="tpu_custom_call" | custom-call | bytes 10485760 | tf_op jit(solution)/shard_map/stage/pallas_call | solution.py:244
  32.0 0.0 collective-permute-done.9.rest_10_
  32.1 0.0 collective-permute-done.4.rest_5_
  32.1 0.0 collective-permute-done.2.rest_3_
  32.1 0.0 collective-permute-done.13.rest_14_
  32.1 1.6 %collective-permute-done.6.rest_7_ = bf16[512,128]{1,0:T(8,128)(2,1)S(1)} collective-permute-done((bf16[512,128]{1,0:T(8,128)(2,1)S(1)}, bf16[512,128]{1,0:T(8,128)(2,1)S(1)}, u32[]{:S(2)}, u32[]{:S(2)}) %collective-permute-start.6) | collective-permute-done | bytes 131104 | tf_op jit(solution)/shard_map/ppermute | solution.py:19
  33.7 0.0 copy-done.6
  33.7 8.9 %attend.1 = (bf16[2,256,512]{2,1,0:T(8,128)(2,1)S(1)}, f32[2,256,512]{2,1,0:T(8,128)S(1)}) custom-call(s32[1,18]{1,0:T(1,128)S(1)} %get-tuple-element.12.table, bf16[256,1024]{1,0:T(8,128)(2,1)S(1)} %get-tuple-element.13.query_ref, bf16[1024,2048]{1,0:T(8,128)(2,1)S(1)} %get-tuple-element.14.proj_ref, bf16[256,128]{1,0:T(8,128)(2,1)S(1)} %get-tuple-element.15.own_keys, ...), custom_call_target="tpu_custom_call" | custom-call | flops 2684354560 | bytes 8388608 | tf_op jit(solution)/shard_map/attend/pallas_call | solution.py:271
  42.6 0.1 collective-permute-start.14
  42.7 1.9 %collective-permute-done.14 = bf16[2,256,512]{2,1,0:T(8,128)(2,1)S(1)} collective-permute-done((bf16[2,256,512]{2,1,0:T(8,128)(2,1)S(1)}, bf16[2,256,512]{2,1,0:T(8,128)(2,1)S(1)}, u32[]{:S(2)}, u32[]{:S(2)}) %collective-permute-start.14) | collective-permute-done | bytes 524320 | tf_op jit(solution)/shard_map/ppermute | solution.py:19
  44.6 0.2 convert_add_fusion
  44.8 1.6 %collective-permute-start.15 = (bf16[1,256,512]{2,1,0:T(8,128)(2,1)S(1)}, bf16[1,256,512]{2,1,0:T(8,128)(2,1)S(1)}, u32[]{:S(2)}, u32[]{:S(2)}) collective-permute-start(bf16[1,256,512]{2,1,0:T(8,128)(2,1)S(1)} %slice.19), channel_id=1, source_target_pairs={{0,2},{1,3},{2,0},{3,1},{4,6},{5,7},{6,4},{7,5},{8,10},{9,11},{10,... | collective-permute-start | bytes 786440 | tf_op jit(solution)/shard_map/ppermute | solution.py:19
  46.4 6.9 %collective-permute-done.15 = bf16[1,256,512]{2,1,0:T(8,128)(2,1)S(1)} collective-permute-done((bf16[1,256,512]{2,1,0:T(8,128)(2,1)S(1)}, bf16[1,256,512]{2,1,0:T(8,128)(2,1)S(1)}, u32[]{:S(2)}, u32[]{:S(2)}) %collective-permute-start.15) | collective-permute-done | bytes 262176 | tf_op jit(solution)/shard_map/ppermute | solution.py:19
  53.2 0.8 %fusion.1 = bf16[256,512]{1,0:T(8,128)(2,1)} fusion(bf16[1,256,512]{2,1,0:T(8,128)(2,1)S(1)} %collective-permute-done.15, f32[2,256,512]{2,1,0:T(8,128)S(1)} %convert_add_fusion), kind=kLoop, calls=%fused_computation.4 | loop fusion | flops 393216 | bytes 1048576 | tf_op jit(solution)/shard_map/convert_element_type | solution.py:305
  (3 shorter events, 0.0 us)
Async XLA Ops:
  0.0 11.9 %collective-permute-start.10 = (bf16[512,128]{1,0:T(8,128)(2,1)}, bf16[512,128]{1,0:T(8,128)(2,1)S(1)}, u32[]{:S(2)}, u32[]{:S(2)}) collective-permute-start(bf16[512,128]{1,0:T(8,128)(2,1)} %bitcast.5), channel_id=1, source_target_pairs={{0,16},{4,20},{8,24},{12,28},{16,0},{20,4},{24,8},{28,12},{1,17},{... | collective-permute-start | bytes 393224 | tf_op jit(solution)/shard_map/ppermute | solution.py:19
  4.1 10.3 %collective-permute-start.8 = (bf16[512,128]{1,0:T(8,128)(2,1)}, bf16[512,128]{1,0:T(8,128)(2,1)S(1)}, u32[]{:S(2)}, u32[]{:S(2)}) collective-permute-start(bf16[512,128]{1,0:T(8,128)(2,1)} %bitcast.6), channel_id=1, source_target_pairs={{0,8},{4,12},{8,0},{12,4},{16,24},{20,28},{24,16},{28,20},{1,9},{5... | collective-permute-start | bytes 393224 | tf_op jit(solution)/shard_map/ppermute | solution.py:19
  5.6 8.7 %collective-permute-start.7 = (bf16[512,128]{1,0:T(8,128)(2,1)}, bf16[512,128]{1,0:T(8,128)(2,1)S(1)}, u32[]{:S(2)}, u32[]{:S(2)}) collective-permute-start(bf16[512,128]{1,0:T(8,128)(2,1)} %bitcast.7), channel_id=1, source_target_pairs={{0,4},{4,0},{8,12},{12,8},{16,20},{20,16},{24,28},{28,24},{1,5},{5... | collective-permute-start | bytes 393224 | tf_op jit(solution)/shard_map/ppermute | solution.py:19
  7.1 9.2 %collective-permute-start.3 = (bf16[512,128]{1,0:T(8,128)(2,1)}, bf16[512,128]{1,0:T(8,128)(2,1)S(1)}, u32[]{:S(2)}, u32[]{:S(2)}) collective-permute-start(bf16[512,128]{1,0:T(8,128)(2,1)} %bitcast.10), channel_id=1, source_target_pairs={{0,16},{4,20},{8,24},{12,28},{16,0},{20,4},{24,8},{28,12},{1,17},{... | collective-permute-start | bytes 393224 | tf_op jit(solution)/shard_map/ppermute | solution.py:19
  7.5 9.8 %collective-permute-start.1 = (bf16[512,128]{1,0:T(8,128)(2,1)}, bf16[512,128]{1,0:T(8,128)(2,1)S(1)}, u32[]{:S(2)}, u32[]{:S(2)}) collective-permute-start(bf16[512,128]{1,0:T(8,128)(2,1)} %bitcast.11), channel_id=1, source_target_pairs={{0,8},{4,12},{8,0},{12,4},{16,24},{20,28},{24,16},{28,20},{1,9},{5... | collective-permute-start | bytes 393224 | tf_op jit(solution)/shard_map/ppermute | solution.py:19
  11.9 7.4 %collective-permute-start = (bf16[512,128]{1,0:T(8,128)(2,1)}, bf16[512,128]{1,0:T(8,128)(2,1)S(1)}, u32[]{:S(2)}, u32[]{:S(2)}) collective-permute-start(bf16[512,128]{1,0:T(8,128)(2,1)} %bitcast.12), channel_id=1, source_target_pairs={{0,4},{4,0},{8,12},{12,8},{16,20},{20,16},{24,28},{28,24},{1,5},{5... | collective-permute-start | bytes 393224 | tf_op jit(solution)/shard_map/ppermute | solution.py:19
  14.3 6.1 %collective-permute-start.12 = (bf16[512,128]{1,0:T(8,128)(2,1)S(1)}, bf16[512,128]{1,0:T(8,128)(2,1)S(1)}, u32[]{:S(2)}, u32[]{:S(2)}) collective-permute-start(bf16[512,128]{1,0:T(8,128)(2,1)S(1)} %collective-permute-done.10.rest_11_), channel_id=1, source_target_pairs={{0,8},{4,12},{8,0},{12,4},{16,24},{20,28},{24,16},{28,20},{1,9},{5... | collective-permute-start | bytes 393224 | tf_op jit(solution)/shard_map/ppermute | solution.py:19
  14.3 7.8 %collective-permute-start.11 = (bf16[512,128]{1,0:T(8,128)(2,1)S(1)}, bf16[512,128]{1,0:T(8,128)(2,1)S(1)}, u32[]{:S(2)}, u32[]{:S(2)}) collective-permute-start(bf16[512,128]{1,0:T(8,128)(2,1)S(1)} %collective-permute-done.10.rest_11_), channel_id=1, source_target_pairs={{0,4},{4,0},{8,12},{12,8},{16,20},{20,16},{24,28},{28,24},{1,5},{5... | collective-permute-start | bytes 393224 | tf_op jit(solution)/shard_map/ppermute | solution.py:19
  16.3 6.2 %collective-permute-start.5 = (bf16[512,128]{1,0:T(8,128)(2,1)S(1)}, bf16[512,128]{1,0:T(8,128)(2,1)S(1)}, u32[]{:S(2)}, u32[]{:S(2)}) collective-permute-start(bf16[512,128]{1,0:T(8,128)(2,1)S(1)} %collective-permute-done.3.rest_4_), channel_id=1, source_target_pairs={{0,8},{4,12},{8,0},{12,4},{16,24},{20,28},{24,16},{28,20},{1,9},{5... | collective-permute-start | bytes 393224 | tf_op jit(solution)/shard_map/ppermute | solution.py:19
  17.3 14.8 %collective-permute-start.4 = (bf16[512,128]{1,0:T(8,128)(2,1)S(1)}, bf16[512,128]{1,0:T(8,128)(2,1)S(1)}, u32[]{:S(2)}, u32[]{:S(2)}) collective-permute-start(bf16[512,128]{1,0:T(8,128)(2,1)S(1)} %collective-permute-done.3.rest_4_), channel_id=1, source_target_pairs={{0,4},{4,0},{8,12},{12,8},{16,20},{20,16},{24,28},{28,24},{1,5},{5... | collective-permute-start | bytes 393224 | tf_op jit(solution)/shard_map/ppermute | solution.py:19
  19.3 12.7 %collective-permute-start.9 = (bf16[512,128]{1,0:T(8,128)(2,1)S(1)}, bf16[512,128]{1,0:T(8,128)(2,1)S(1)}, u32[]{:S(2)}, u32[]{:S(2)}) collective-permute-start(bf16[512,128]{1,0:T(8,128)(2,1)S(1)} %collective-permute-done.8.rest_9_), channel_id=1, source_target_pairs={{0,4},{4,0},{8,12},{12,8},{16,20},{20,16},{24,28},{28,24},{1,5},{5... | collective-permute-start | bytes 393224 | tf_op jit(solution)/shard_map/ppermute | solution.py:19
  20.5 11.6 %collective-permute-start.2 = (bf16[512,128]{1,0:T(8,128)(2,1)S(1)}, bf16[512,128]{1,0:T(8,128)(2,1)S(1)}, u32[]{:S(2)}, u32[]{:S(2)}) collective-permute-start(bf16[512,128]{1,0:T(8,128)(2,1)S(1)} %collective-permute-done.1.rest_2_), channel_id=1, source_target_pairs={{0,4},{4,0},{8,12},{12,8},{16,20},{20,16},{24,28},{28,24},{1,5},{5... | collective-permute-start | bytes 393224 | tf_op jit(solution)/shard_map/ppermute | solution.py:19
  22.1 10.0 %collective-permute-start.13 = (bf16[512,128]{1,0:T(8,128)(2,1)S(1)}, bf16[512,128]{1,0:T(8,128)(2,1)S(1)}, u32[]{:S(2)}, u32[]{:S(2)}) collective-permute-start(bf16[512,128]{1,0:T(8,128)(2,1)S(1)} %collective-permute-done.12.rest_13_), channel_id=1, source_target_pairs={{0,4},{4,0},{8,12},{12,8},{16,20},{20,16},{24,28},{28,24},{1,5},{5... | collective-permute-start | bytes 393224 | tf_op jit(solution)/shard_map/ppermute | solution.py:19
  22.5 11.2 %collective-permute-start.6 = (bf16[512,128]{1,0:T(8,128)(2,1)S(1)}, bf16[512,128]{1,0:T(8,128)(2,1)S(1)}, u32[]{:S(2)}, u32[]{:S(2)}) collective-permute-start(bf16[512,128]{1,0:T(8,128)(2,1)S(1)} %collective-permute-done.5.rest_6_), channel_id=1, source_target_pairs={{0,4},{4,0},{8,12},{12,8},{16,20},{20,16},{24,28},{28,24},{1,5},{5... | collective-permute-start | bytes 393224 | tf_op jit(solution)/shard_map/ppermute | solution.py:19
  24.2 2.2 %copy-start = (bf16[1024,2048]{1,0:T(8,128)(2,1)S(1)}, bf16[1024,2048]{1,0:T(8,128)(2,1)}, u32[]{:S(2)}) copy-start(bf16[1024,2048]{1,0:T(8,128)(2,1)} %proj_in.1) | copy-start | bytes 12582916
  26.4 1.0 %copy-start.1 = (bf16[256,1024]{1,0:T(8,128)(2,1)S(1)}, bf16[256,1024]{1,0:T(8,128)(2,1)}, u32[]{:S(2)}) copy-start(bf16[256,1024]{1,0:T(8,128)(2,1)} %query_in.1) | copy-start | bytes 1572868
  27.4 0.9 %copy-start.2 = (bf16[256,2,128]{2,1,0:T(2,128)(2,1)S(1)}, bf16[256,2,128]{2,1,0:T(2,128)(2,1)}, u32[]{:S(2)}) copy-start(bf16[256,2,128]{2,1,0:T(2,128)(2,1)} %param.8) | copy-start | bytes 393220
  28.3 0.7 %copy-start.3 = (s32[1,4]{1,0:T(1,128)S(1)}, s32[1,4]{1,0:T(1,128)}, u32[]{:S(2)}) copy-start(s32[1,4]{1,0:T(1,128)} %page_ref.1) | copy-start | bytes 52
  29.0 0.7 %copy-start.4 = (s32[1,3]{1,0:T(1,128)S(1)}, s32[1,3]{1,0:T(1,128)}, u32[]{:S(2)}) copy-start(s32[1,3]{1,0:T(1,128)} %shift_ref.1) | copy-start | bytes 40
  29.6 0.7 %copy-start.5 = (s32[1,1,3]{2,1,0:T(1,128)S(1)}, s32[1,1,3]{2,1,0:T(1,128)}, u32[]{:S(2)}) copy-start(s32[1,1,3]{2,1,0:T(1,128)} %param.12) | copy-start | bytes 40
  30.3 3.5 %copy-start.6 = (bf16[256,2,128]{2,1,0:T(2,128)(2,1)S(1)}, bf16[256,2,128]{2,1,0:T(2,128)(2,1)}, u32[]{:S(2)}) copy-start(bf16[256,2,128]{2,1,0:T(2,128)(2,1)} %param.9) | copy-start | bytes 393220
  42.6 2.0 %collective-permute-start.14 = (bf16[2,256,512]{2,1,0:T(8,128)(2,1)S(1)}, bf16[2,256,512]{2,1,0:T(8,128)(2,1)S(1)}, u32[]{:S(2)}, u32[]{:S(2)}) collective-permute-start(bf16[2,256,512]{2,1,0:T(8,128)(2,1)S(1)} %get-tuple-element.18), channel_id=1, source_target_pairs={{0,1},{1,0},{2,3},{3,2},{4,5},{5,4},{6,7},{7,6},{8,9},{9,8},{10,11... | collective-permute-start | bytes 1572872 | tf_op jit(solution)/shard_map/ppermute | solution.py:19
  44.8 8.4 %collective-permute-start.15 = (bf16[1,256,512]{2,1,0:T(8,128)(2,1)S(1)}, bf16[1,256,512]{2,1,0:T(8,128)(2,1)S(1)}, u32[]{:S(2)}, u32[]{:S(2)}) collective-permute-start(bf16[1,256,512]{2,1,0:T(8,128)(2,1)S(1)} %slice.19), channel_id=1, source_target_pairs={{0,2},{1,3},{2,0},{3,1},{4,6},{5,7},{6,4},{7,5},{8,10},{9,11},{10,... | collective-permute-start | bytes 786440 | tf_op jit(solution)/shard_map/ppermute | solution.py:19
